TPU v7x, 32 devices: a whole 2x2x4 slice. The times are simulated.
32 devices in a mesh: dp: 8 (over z, x), tensor: 4 (over y, core).
Axes of the slice: x: 2, y: 2, z: 4, core: 2. Of those that a mesh axis runs over, the one named last changes fastest.
Arguments:
- hidden_in: bfloat16 [8192, 768], P('dp'), may hold values from -6 to 6
- w_qkv: bfloat16 [3, 768, 768], P(None, None, 'tensor'), may hold values from -0.21875 to 0.21875
- w_out: bfloat16 [768, 768], P('tensor'), may hold values from -0.625 to 0.625
- w_ff1: bfloat16 [768, 768], P(None, 'tensor'), may hold values from -0.21875 to 0.21875
- w_ff2: bfloat16 [768, 768], P('tensor'), may hold values from -0.21875 to 0.21875
- ln1_gain: float32 [768], replicated, may hold values from 0.5 to 1.5
- ln1_bias: float32 [768], replicated, may hold values from -3 to 3
- ln2_gain: float32 [768], replicated, may hold values from 0.5 to 1.5
- ln2_bias: float32 [768], replicated, may hold values from -3 to 3
- spd_table: float32 [32, 32], P(None, 'tensor'), may hold values from -3 to 3
- edge_table: float32 [32, 32], P(None, 'tensor'), may hold values from -3 to 3
- kernel_w1: bfloat16 [128, 128], replicated, may hold values from -0.5 to 0.5
- kernel_w2: bfloat16 [128, 32], P(None, 'tensor'), may hold values from -0.5 to 0.5
- centers: float32 [128], replicated, may hold values from 0 to 8
- widths: float32 [128], replicated, may hold values from 0.3 to 3
- atom_count: int32 [128], P('dp'), may hold values from 16 to 64, as said below
- mol_mode: int32 [128], P('dp'), may hold values from 0 to 2
- spd_bucket: int32 [128, 64, 64], P('dp'), may hold values from 0 to 31
- edge_type: int32 [128, 64, 64], P('dp'), may hold values from 0 to 31
- dist_bucket: int32 [128, 64, 64], P('dp'), may hold values from 0 to 127
- cotangent: bfloat16 [8192, 768], P('dp'), may hold values from -6 to 6
Outputs:
- layer_out: bfloat16 [8192, 768], P('dp')
- grad_in: bfloat16 [8192, 768], P('dp')
- grad_qkv: float32 [3, 768, 768], P(None, None, 'tensor')
- grad_out: float32 [768, 768], P('tensor')
- grad_ff1: float32 [768, 768], P(None, 'tensor')
- grad_ff2: float32 [768, 768], P('tensor')
- grad_ln1_gain: float32 [768], replicated
- grad_ln1_bias: float32 [768], replicated
- grad_ln2_gain: float32 [768], replicated
- grad_ln2_bias: float32 [768], replicated
- grad_spd: float32 [32, 32], P(None, 'tensor')
- grad_edge: float32 [32, 32], P(None, 'tensor')
- grad_kernel_w1: float32 [128, 128], replicated
- grad_kernel_w2: float32 [128, 32], P(None, 'tensor')
- grad_centers: float32 [128], replicated
- grad_widths: float32 [128], replicated
Inputs may be any that keep to these rules, and one draw needn't show every extreme that they name: `atom_count`: every molecule has at least 16 real atoms, and some molecule has exactly 64.
All inputs are finite; a program needn't handle non-finite values.
Results may differ from a plain program's by a relative error of at most 0.02.
Values may be sent and summed in bfloat16 or wider, within the bound.
No kernel may reach another device: no remote copies, remote signals or barrier semaphores. Data moves between devices by JAX's collectives and lax.ppermute only.
A program may use at most 128 MiB of HBM per device.

v0:
```python
from functools import partial
import math

import jax
import jax.numpy as jnp
from jax import lax
from jax.sharding import PartitionSpec as P

DIST = 128


eps = 1e-05
neg_fill = -1000000000.0
highest = lax.Precision.HIGHEST


def norm_rows(values, gain, shift):
    center = values - jnp.mean(values, axis=-1, keepdims=True)
    spread = jnp.mean(center * center, axis=-1, keepdims=True)
    return center * lax.rsqrt(spread + eps) * gain + shift


def gelu_exact(values):
    return jax.nn.gelu(values, approximate=False)


def kernels(dist, centers, widths):
    place = dist.astype(jnp.float32)[..., None] * (8.0 / DIST)
    offset = (place - centers) / widths
    return jnp.exp(-0.5 * offset * offset) / widths


def kernel_geo(weights, dist_rows):
    kernel_w1, kernel_w2, centers, widths = weights
    total = dist_rows.shape[0]
    block = math.gcd(total, 16384)

    def one_block(rows):
        basis = kernels(rows, centers, widths).astype(jnp.bfloat16)
        inner = jnp.dot(basis, kernel_w1, preferred_element_type=jnp.float32)
        hidden = gelu_exact(inner).astype(jnp.bfloat16)
        return jnp.dot(hidden, kernel_w2, preferred_element_type=jnp.float32)

    result = lax.map(one_block, dist_rows.reshape(total // block, block))
    return result.reshape(total, kernel_w2.shape[1])


def kernel_grads(weights, dist_rows, grad_geo):
    kernel_w1, kernel_w2, centers, widths = weights
    total = dist_rows.shape[0]
    block = math.gcd(total, 16384)

    def one_block(carry, items):
        acc_one, acc_two, acc_center, acc_width = carry
        rows, grad_rows = items
        basis, basis_pull = jax.vjp(lambda cen, wid: kernels(rows, cen, wid), centers, widths)
        basis_b = basis.astype(jnp.bfloat16)
        inner = jnp.dot(basis_b, kernel_w1, preferred_element_type=jnp.float32)
        hidden, gelu_pull = jax.vjp(gelu_exact, inner)
        hidden_b = hidden.astype(jnp.bfloat16)
        acc_two = acc_two + jnp.dot(hidden_b.T, grad_rows, preferred_element_type=jnp.float32)
        grad_hidden = jnp.dot(grad_rows, kernel_w2.T, preferred_element_type=jnp.float32)
        grad_inner = gelu_pull(grad_hidden)[0].astype(jnp.bfloat16)
        acc_one = acc_one + jnp.dot(basis_b.T, grad_inner, preferred_element_type=jnp.float32)
        grad_basis = jnp.dot(grad_inner, kernel_w1.T, preferred_element_type=jnp.float32)
        grad_center, grad_width = basis_pull(grad_basis)
        return ((acc_one, acc_two, acc_center + grad_center, acc_width + grad_width), None)

    start_carry = (
        jnp.zeros(kernel_w1.shape, jnp.float32),
        jnp.zeros(kernel_w2.shape, jnp.float32),
        jnp.zeros(centers.shape, jnp.float32),
        jnp.zeros(widths.shape, jnp.float32),
    )
    result, unused = lax.scan(
        one_block,
        start_carry,
        (
            dist_rows.reshape(total // block, block),
            grad_geo.reshape(total // block, block, grad_geo.shape[1]),
        ),
    )
    return result


def block_bias(tables, mode, spd_ids, edge_ids, geo):
    spd_table, edge_table = tables
    spd_hot = jax.nn.one_hot(spd_ids, spd_table.shape[0], dtype=jnp.float32)
    edge_hot = jax.nn.one_hot(edge_ids, edge_table.shape[0], dtype=jnp.float32)
    flat = jnp.dot(spd_hot, spd_table, precision=highest) + jnp.dot(
        edge_hot, edge_table, precision=highest
    )
    two_flag = (mode != 1).astype(jnp.float32)[:, None, None, None]
    three_flag = (mode != 0).astype(jnp.float32)[:, None, None, None]
    return (two_flag * flat + three_flag * geo, spd_hot, edge_hot, two_flag, three_flag)


def scores_of(query, keyset, bias, count):
    atoms = query.shape[1]
    scores = jnp.einsum("bihe,bjhe->bhij", query, keyset, preferred_element_type=jnp.float32)
    scores = scores + jnp.transpose(bias, (0, 3, 1, 2))
    keep = (jnp.arange(atoms)[None, :] < count[:, None])[:, None, None, :]
    return jnp.where(keep, scores, neg_fill)


def attend(tables, items):
    query, keyset, values, count, mode, spd_ids, edge_ids, geo = items
    bias = block_bias(tables, mode, spd_ids, edge_ids, geo)[0]
    scores = scores_of(query, keyset, bias, count)
    row_max = jnp.max(scores, axis=-1, keepdims=True)
    expos = jnp.exp(scores - row_max)
    totals = jnp.sum(expos, axis=-1, keepdims=True)
    probs = (expos / totals).astype(jnp.bfloat16)
    mixed = jnp.einsum("bhij,bjhe->bihe", probs, values, preferred_element_type=jnp.float32)
    return (mixed.astype(jnp.bfloat16), row_max + jnp.log(totals))


def attend_back(tables, carry, items):
    query, keyset, values, grad_mixed, log_sums, count, mode, spd_ids, edge_ids, geo = items
    acc_spd, acc_edge = carry
    bias, spd_hot, edge_hot, two_flag, three_flag = block_bias(tables, mode, spd_ids, edge_ids, geo)
    scores = scores_of(query, keyset, bias, count)
    probs = jnp.exp(scores - log_sums)
    grad_values = jnp.einsum(
        "bhij,bihe->bjhe",
        probs.astype(jnp.bfloat16),
        grad_mixed,
        preferred_element_type=jnp.float32,
    )
    grad_probs = jnp.einsum(
        "bihe,bjhe->bhij", grad_mixed, values, preferred_element_type=jnp.float32
    )
    grad_scores = probs * (grad_probs - jnp.sum(probs * grad_probs, axis=-1, keepdims=True))
    grad_scores = grad_scores.astype(jnp.bfloat16)
    grad_query = jnp.einsum(
        "bhij,bjhe->bihe", grad_scores, keyset, preferred_element_type=jnp.float32
    )
    grad_keys = jnp.einsum(
        "bhij,bihe->bjhe", grad_scores, query, preferred_element_type=jnp.float32
    )
    grad_bias = jnp.transpose(grad_scores, (0, 2, 3, 1))
    flat_grad = two_flag.astype(jnp.bfloat16) * grad_bias
    acc_spd = acc_spd + jnp.einsum(
        "bijs,bijh->sh", spd_hot.astype(jnp.bfloat16), flat_grad, preferred_element_type=jnp.float32
    )
    acc_edge = acc_edge + jnp.einsum(
        "bijs,bijh->sh",
        edge_hot.astype(jnp.bfloat16),
        flat_grad,
        preferred_element_type=jnp.float32,
    )
    geo_grad = three_flag.astype(jnp.bfloat16) * grad_bias
    outputs = (
        grad_query.astype(jnp.bfloat16),
        grad_keys.astype(jnp.bfloat16),
        grad_values.astype(jnp.bfloat16),
        geo_grad,
    )
    return ((acc_spd, acc_edge), outputs)


def gain_grads(values, gain, shift, grad_rows):
    pull = jax.vjp(norm_rows, values, gain, shift)[1]
    return pull(grad_rows)


def body(
    hidden_in,
    w_qkv,
    w_out,
    w_ff1,
    w_ff2,
    ln1_gain,
    ln1_bias,
    ln2_gain,
    ln2_bias,
    spd_table,
    edge_table,
    kernel_w1,
    kernel_w2,
    centers,
    widths,
    atom_count,
    mol_mode,
    spd_bucket,
    edge_type,
    dist_bucket,
    cotangent,
):
    tokens = hidden_in.shape[0]
    mols, atoms = (spd_bucket.shape[0], spd_bucket.shape[1])
    heads_here = spd_table.shape[1]
    columns = w_qkv.shape[2]
    head_dim = columns // heads_here
    group = math.gcd(mols, max(1, 2048 // atoms))
    count_blocks = mols // group
    scale = 1.0 / math.sqrt(head_dim)
    tables = (spd_table, edge_table)
    pairs = mols * atoms * atoms
    dist_rows = dist_bucket.reshape(pairs)

    def by_block(array):
        return array.reshape((count_blocks, group) + array.shape[1:])

    def heads_view(array):
        return array.reshape(count_blocks, group, atoms, heads_here, head_dim)

    source = hidden_in.astype(jnp.float32)
    upstream = cotangent.astype(jnp.float32)
    share_rows = tokens // lax.axis_size("tensor")
    start = lax.axis_index("tensor") * share_rows
    source_share = lax.dynamic_slice_in_dim(source, start, share_rows, 0)
    geo = kernel_geo((kernel_w1, kernel_w2, centers, widths), dist_rows)
    geo_view = geo.reshape(count_blocks, group, atoms, atoms, heads_here)
    normed_one = norm_rows(source, ln1_gain, ln1_bias).astype(jnp.bfloat16)
    projected = jnp.einsum("td,kdc->ktc", normed_one, w_qkv, preferred_element_type=jnp.float32)
    query_b = (projected[0] * scale).astype(jnp.bfloat16)
    key_b = projected[1].astype(jnp.bfloat16)
    value_b = projected[2].astype(jnp.bfloat16)
    int_items = (
        by_block(atom_count),
        by_block(mol_mode),
        by_block(spd_bucket),
        by_block(edge_type),
        geo_view,
    )
    attended, log_sums = lax.map(
        partial(attend, tables),
        (heads_view(query_b), heads_view(key_b), heads_view(value_b)) + int_items,
    )
    attended = attended.reshape(tokens, columns)
    attn_part = jnp.dot(attended, w_out, preferred_element_type=jnp.float32)
    middle = source + lax.psum(attn_part.astype(jnp.bfloat16), "tensor").astype(jnp.float32)
    normed_two = norm_rows(middle, ln2_gain, ln2_bias).astype(jnp.bfloat16)
    inner = jnp.dot(normed_two, w_ff1, preferred_element_type=jnp.float32)
    active = gelu_exact(inner).astype(jnp.bfloat16)
    ffn_part = jnp.dot(active, w_ff2, preferred_element_type=jnp.float32)
    layer_out = (
        middle + lax.psum(ffn_part.astype(jnp.bfloat16), "tensor").astype(jnp.float32)
    ).astype(jnp.bfloat16)
    grad_ff2 = jnp.dot(active.T, cotangent, preferred_element_type=jnp.float32)
    grad_active = jnp.dot(cotangent, w_ff2.T, preferred_element_type=jnp.float32)
    gelu_pull = jax.vjp(gelu_exact, inner)[1]
    grad_inner = gelu_pull(grad_active)[0].astype(jnp.bfloat16)
    grad_ff1 = jnp.dot(normed_two.T, grad_inner, preferred_element_type=jnp.float32)
    two_part = jnp.dot(grad_inner, w_ff1.T, preferred_element_type=jnp.float32)
    two_grad = lax.psum(two_part.astype(jnp.bfloat16), "tensor").astype(jnp.float32)
    back_middle = gain_grads(middle, ln2_gain, ln2_bias, two_grad)[0]
    middle_share = lax.dynamic_slice_in_dim(middle, start, share_rows, 0)
    two_share = lax.dynamic_slice_in_dim(two_grad, start, share_rows, 0)
    unused, grad_g2, grad_b2 = gain_grads(middle_share, ln2_gain, ln2_bias, two_share)
    middle_grad = upstream + back_middle
    middle_grad_b = middle_grad.astype(jnp.bfloat16)
    grad_out = jnp.dot(attended.T, middle_grad_b, preferred_element_type=jnp.float32)
    grad_attended = jnp.dot(middle_grad_b, w_out.T, preferred_element_type=jnp.float32).astype(
        jnp.bfloat16
    )
    carry_start = (
        jnp.zeros(spd_table.shape, jnp.float32),
        jnp.zeros(edge_table.shape, jnp.float32),
    )
    table_grads, back_outs = lax.scan(
        partial(attend_back, tables),
        carry_start,
        (
            heads_view(query_b),
            heads_view(key_b),
            heads_view(value_b),
            heads_view(grad_attended),
            log_sums,
        )
        + int_items,
    )
    grad_spd, grad_edge = table_grads
    geo_grad = back_outs[3].reshape(pairs, heads_here)
    grad_kw1, grad_kw2, grad_cen, grad_wid = kernel_grads(
        (kernel_w1, kernel_w2, centers, widths), dist_rows, geo_grad
    )
    grad_qkv_b = jnp.stack(
        [
            back_outs[0].reshape(tokens, columns),
            back_outs[1].reshape(tokens, columns),
            back_outs[2].reshape(tokens, columns),
        ]
    )
    factor = jnp.array([scale, 1.0, 1.0], jnp.float32)[:, None, None]
    grad_qkv = (
        jnp.einsum("td,ktc->kdc", normed_one, grad_qkv_b, preferred_element_type=jnp.float32)
        * factor
    )
    one_parts = jnp.einsum("ktc,kdc->ktd", grad_qkv_b, w_qkv, preferred_element_type=jnp.float32)
    one_part = jnp.sum(one_parts * factor, axis=0)
    one_grad = lax.psum(one_part.astype(jnp.bfloat16), "tensor").astype(jnp.float32)
    back_source = gain_grads(source, ln1_gain, ln1_bias, one_grad)[0]
    one_share = lax.dynamic_slice_in_dim(one_grad, start, share_rows, 0)
    unused, grad_g1, grad_b1 = gain_grads(source_share, ln1_gain, ln1_bias, one_share)
    grad_in = (middle_grad + back_source).astype(jnp.bfloat16)
    sharded = (
        lax.psum(grad_qkv.astype(jnp.bfloat16), "dp").astype(jnp.float32),
        lax.psum(grad_out.astype(jnp.bfloat16), "dp").astype(jnp.float32),
        lax.psum(grad_ff1.astype(jnp.bfloat16), "dp").astype(jnp.float32),
        lax.psum(grad_ff2.astype(jnp.bfloat16), "dp").astype(jnp.float32),
        lax.psum(grad_spd.astype(jnp.bfloat16), "dp").astype(jnp.float32),
        lax.psum(grad_edge.astype(jnp.bfloat16), "dp").astype(jnp.float32),
        lax.psum(grad_kw2.astype(jnp.bfloat16), "dp").astype(jnp.float32),
    )
    shared = lax.psum(
        (grad_kw1, grad_cen, grad_wid, grad_g1, grad_b1, grad_g2, grad_b2), ("dp", "tensor")
    )
    return (
        layer_out,
        grad_in,
        sharded[0],
        sharded[1],
        sharded[2],
        sharded[3],
        shared[3],
        shared[4],
        shared[5],
        shared[6],
        sharded[4],
        sharded[5],
        shared[0],
        sharded[6],
        shared[1],
        shared[2],
    )


def solution(mesh):
    in_specs = (
        P("dp", None),
        P(None, None, "tensor"),
        P("tensor", None),
        P(None, "tensor"),
        P("tensor", None),
        P(),
        P(),
        P(),
        P(),
        P(None, "tensor"),
        P(None, "tensor"),
        P(),
        P(None, "tensor"),
        P(),
        P(),
        P("dp"),
        P("dp"),
        P("dp", None, None),
        P("dp", None, None),
        P("dp", None, None),
        P("dp", None),
    )
    out_specs = (
        P("dp", None),
        P("dp", None),
        P(None, None, "tensor"),
        P("tensor", None),
        P(None, "tensor"),
        P("tensor", None),
        P(),
        P(),
        P(),
        P(),
        P(None, "tensor"),
        P(None, "tensor"),
        P(),
        P(None, "tensor"),
        P(),
        P(),
    )
    return jax.shard_map(body, mesh=mesh, in_specs=in_specs, out_specs=out_specs, check_vma=False)
```

profile of v0, /device:TPU:0, one launch (start us, length us, event | category | flops | bytes accessed | tf_op | source)
XLA Modules:
  0.0 701.5 jit_solution(9813940309770022953)
XLA Ops:
  17.9 129.4 %while.6 = (s32[]{:T(128)}, f32[4,16384,8]{1,0,2:T(4,128)}, s32[4,16384]{1,0:T(4,128)S(1)}, f32[128]{0:T(128)S(1)}, f32[128]{0:T(128)S(1)}, /*index=5*/bf16[128,...) while((s32[]{:T(128)}, f32[4,16384,8]{1,0,2:T(4,128)}, s32[4,16384]{1,0:T(4,128)S(1)}, ...), condition=%wide.region_3.4_spmd, body=%wide.region_2.3_spmd.sunk | while | flops 719355904 | bytes 2853997 | solution.py:44
  18.3 21.2 %convolution_bitcast_fusion.2 = f32[1,16384,8]{1,2,0:T(8,128)S(1)} fusion(bf16[128,8]{0,1:T(8,128)(2,1)S(1)} %get-tuple-element.560, bf16[128,128]{1,0:T(8,128)(2,1)S(1)} %get-tuple-element.559, f32[128]{0:T(128)S(1)} %get-tuple-element.558, f32[128]{0:T(128)S(1)} %get-tuple-element.557, f32[16384]{0:T(1024)S(1)} %bitcast.180), kind=kOutput, calls=%fused_computation.clone.1 | convolution fusion | flops 719323136 | bytes 625664 | tf_op jit(solution)/shard_map/while/body/eval_jaxpr/dot_general | solution.py:42
  40.0 10.5 %dynamic_update_slice.20 = f32[4,16384,8]{1,0,2:T(4,128)} dynamic-update-slice(f32[4,16384,8]{1,0,2:T(4,128)} %get-tuple-element.546, f32[1,16384,8]{1,0,2:T(1,128)S(1)} %copy.132, s32[]{:T(128)S(6)} %copy.136, s32[]{:T(128)} %constant.311.clone.1..sunk, s32[]{:T(128)} %constant.311.clone.1..sunk) | dynamic-update-slice | bytes 1048580 | tf_op jit(solution)/shard_map/while/body/jit(dynamic_update_index_in_dim)/dynamic_update_slice | solution.py:44
  50.6 21.2 %convolution_bitcast_fusion.2 = f32[1,16384,8]{1,2,0:T(8,128)S(1)} fusion(bf16[128,8]{0,1:T(8,128)(2,1)S(1)} %get-tuple-element.560, bf16[128,128]{1,0:T(8,128)(2,1)S(1)} %get-tuple-element.559, f32[128]{0:T(128)S(1)} %get-tuple-element.558, f32[128]{0:T(128)S(1)} %get-tuple-element.557, f32[16384]{0:T(1024)S(1)} %bitcast.180), kind=kOutput, calls=%fused_computation.clone.1 | convolution fusion | flops 719323136 | bytes 625664 | tf_op jit(solution)/shard_map/while/body/eval_jaxpr/dot_general | solution.py:42
  72.3 10.5 %dynamic_update_slice.20 = f32[4,16384,8]{1,0,2:T(4,128)} dynamic-update-slice(f32[4,16384,8]{1,0,2:T(4,128)} %get-tuple-element.546, f32[1,16384,8]{1,0,2:T(1,128)S(1)} %copy.132, s32[]{:T(128)S(6)} %copy.136, s32[]{:T(128)} %constant.311.clone.1..sunk, s32[]{:T(128)} %constant.311.clone.1..sunk) | dynamic-update-slice | bytes 1048580 | tf_op jit(solution)/shard_map/while/body/jit(dynamic_update_index_in_dim)/dynamic_update_slice | solution.py:44
  82.8 21.2 %convolution_bitcast_fusion.2 = f32[1,16384,8]{1,2,0:T(8,128)S(1)} fusion(bf16[128,8]{0,1:T(8,128)(2,1)S(1)} %get-tuple-element.560, bf16[128,128]{1,0:T(8,128)(2,1)S(1)} %get-tuple-element.559, f32[128]{0:T(128)S(1)} %get-tuple-element.558, f32[128]{0:T(128)S(1)} %get-tuple-element.557, f32[16384]{0:T(1024)S(1)} %bitcast.180), kind=kOutput, calls=%fused_computation.clone.1 | convolution fusion | flops 719323136 | bytes 625664 | tf_op jit(solution)/shard_map/while/body/eval_jaxpr/dot_general | solution.py:42
  104.5 10.5 %dynamic_update_slice.20 = f32[4,16384,8]{1,0,2:T(4,128)} dynamic-update-slice(f32[4,16384,8]{1,0,2:T(4,128)} %get-tuple-element.546, f32[1,16384,8]{1,0,2:T(1,128)S(1)} %copy.132, s32[]{:T(128)S(6)} %copy.136, s32[]{:T(128)} %constant.311.clone.1..sunk, s32[]{:T(128)} %constant.311.clone.1..sunk) | dynamic-update-slice | bytes 1048580 | tf_op jit(solution)/shard_map/while/body/jit(dynamic_update_index_in_dim)/dynamic_update_slice | solution.py:44
  115.1 21.2 %convolution_bitcast_fusion.2 = f32[1,16384,8]{1,2,0:T(8,128)S(1)} fusion(bf16[128,8]{0,1:T(8,128)(2,1)S(1)} %get-tuple-element.560, bf16[128,128]{1,0:T(8,128)(2,1)S(1)} %get-tuple-element.559, f32[128]{0:T(128)S(1)} %get-tuple-element.558, f32[128]{0:T(128)S(1)} %get-tuple-element.557, f32[16384]{0:T(1024)S(1)} %bitcast.180), kind=kOutput, calls=%fused_computation.clone.1 | convolution fusion | flops 719323136 | bytes 625664 | tf_op jit(solution)/shard_map/while/body/eval_jaxpr/dot_general | solution.py:42
  136.8 10.5 %dynamic_update_slice.20 = f32[4,16384,8]{1,0,2:T(4,128)} dynamic-update-slice(f32[4,16384,8]{1,0,2:T(4,128)} %get-tuple-element.546, f32[1,16384,8]{1,0,2:T(1,128)S(1)} %copy.132, s32[]{:T(128)S(6)} %copy.136, s32[]{:T(128)} %constant.311.clone.1..sunk, s32[]{:T(128)} %constant.311.clone.1..sunk) | dynamic-update-slice | bytes 1048580 | tf_op jit(solution)/shard_map/while/body/jit(dynamic_update_index_in_dim)/dynamic_update_slice | solution.py:44
  148.0 5.3 squeeze.56
  153.3 5.5 copy.59
  163.7 7.7 %fusion.83 = f32[16,64,64,8]{2,3,1,0:T(8,128)} fusion(s32[16,64,64]{2,1,0:T(8,128)} %param.43, f32[32,8]{0,1:T(8,128)S(1)} %copy-done.68), kind=kOutput, calls=%fused_computation.114 | convolution fusion | flops 203423744 | bytes 2360320 | tf_op jit(solution)/shard_map/while/body/eval_jaxpr/dot_general | solution.py:90
  171.5 5.4 copy.56
  176.8 7.5 %fusion.82 = f32[16,64,64,8]{2,3,1,0:T(8,128)} fusion(s32[16,64,64]{2,1,0:T(8,128)} %param.44, f32[32,8]{0,1:T(8,128)S(1)} %copy-done.69), kind=kOutput, calls=%fused_computation.112 | convolution fusion | flops 203423744 | bytes 2360320 | tf_op jit(solution)/shard_map/while/body/eval_jaxpr/dot_general | solution.py:90
  184.3 5.4 copy.57
  189.7 8.0 %fusion.153 = (f32[16,8,64]{2,1,0:T(8,128)S(1)}, f32[16,8,64,64]{2,3,1,0:T(8,128)S(1)}, f32[16,64,64,8]{1,2,3,0:T(8,128)}, f32[16,8,64,64]{2,3,1,0:T(8,128)}) fusion(pred[16,64]{1,0:T(8,128)(4,1)S(1)} %copy-done.61, f32[16,64,64,8]{1,2,3,0:T(8,128)} %copy.59, f32[16]{0:T(128)S(1)} %copy-done.75, f32[16,64,64,8]{1,2,3,0:T(8,128)} %copy.56, ...), kind=kOutput, calls=%fused_computation.248 | convolution fusion | flops 28827648 | bytes 13403264 | tf_op jit(solution)/shard_map/while/body/eval_jaxpr/bihe,bjhe->bhij/dot_general | solution.py:100
  211.9 40.5 %all-reduce.10.cloned.1.call-done = bf16[1024,768]{1,0:T(8,128)(2,1)} async-done(((bf16[1024,768]{1,0:T(8,128)(2,1)}), bf16[1024,768]{1,0:T(8,128)(2,1)}) %all-reduce.10.cloned.1.call-update) | async-done | bytes 1572880 | tf_op jit(solution)/shard_map/psum | solution.py:233
  275.6 36.9 %all-reduce.12.cloned.1.call-done = bf16[1024,768]{1,0:T(8,128)(2,1)} async-done(((bf16[1024,768]{1,0:T(8,128)(2,1)}), bf16[1024,768]{1,0:T(8,128)(2,1)}) %all-reduce.12.cloned.1.call-update) | async-done | bytes 1572880 | tf_op jit(solution)/shard_map/psum | solution.py:247
  354.1 6.6 broadcast_multiply_fusion.1
  376.5 165.0 %while.7 = (s32[]{:T(128)}, f32[128,128]{1,0:T(8,128)S(1)}, f32[128,8]{0,1:T(8,128)S(1)}, f32[128]{0:T(128)}, f32[128]{0:T(128)}, /*index=5*/s32[4,16384]{1,0:T(...) while((s32[]{:T(128)}, f32[128,128]{1,0:T(8,128)S(1)}, ...), condition=%wide.region_40.41_spmd.clone, body=%wide.region_36.40_spmd.clone.sunk | while | flops 1914768128 | bytes 101811056 | solution.py:75
  377.8 19.5 %fusion.218 = (f32[16384,128]{1,0:T(8,128)S(1)}, f32[16384,128]{1,0:T(8,128)S(1)}) fusion(bf16[128,128]{1,0:T(8,128)(2,1)S(1)} %get-tuple-element.599, f32[128]{0:T(128)S(1)} %get-tuple-element.598, f32[128]{0:T(128)S(1)} %get-tuple-element.597, f32[16384]{0:T(1024)S(1)} %bitcast.173), kind=kOutput, calls=%fused_computation.69.clone.1 | convolution fusion | flops 679477248 | bytes 16876544 | tf_op jit(solution)/shard_map/while/body/eval_jaxpr/dot_general | solution.py:58
  409.8 7.4 %fusion.222 = (f32[128]{0:T(128)S(1)}, f32[128]{0:T(128)S(1)}, f32[128]{0:T(128)S(1)}) fusion(f32[16384,128]{1,0:T(8,128)S(1)} %get-tuple-element.529, f32[128]{0:T(128)S(1)} %divide_bitcast_fusion.2, f32[128]{0:T(128)S(1)} %get-tuple-element.597, f32[16384]{0:T(1024)S(1)} %bitcast.176, f32[128]{0:T(128)S(1)} %get-tuple-element.598, ...), kind=kLoop, calls=%fused_computation.66.clone.1 | loop fusion | flops 25165440 | bytes 16845824 | tf_op jit(solution)/shard_map/while/body/eval_jaxpr/transpose(jvp())/reduce_sum | solution.py:29
  418.9 19.5 %fusion.218 = (f32[16384,128]{1,0:T(8,128)S(1)}, f32[16384,128]{1,0:T(8,128)S(1)}) fusion(bf16[128,128]{1,0:T(8,128)(2,1)S(1)} %get-tuple-element.599, f32[128]{0:T(128)S(1)} %get-tuple-element.598, f32[128]{0:T(128)S(1)} %get-tuple-element.597, f32[16384]{0:T(1024)S(1)} %bitcast.173), kind=kOutput, calls=%fused_computation.69.clone.1 | convolution fusion | flops 679477248 | bytes 16876544 | tf_op jit(solution)/shard_map/while/body/eval_jaxpr/dot_general | solution.py:58
  451.0 7.4 %fusion.222 = (f32[128]{0:T(128)S(1)}, f32[128]{0:T(128)S(1)}, f32[128]{0:T(128)S(1)}) fusion(f32[16384,128]{1,0:T(8,128)S(1)} %get-tuple-element.529, f32[128]{0:T(128)S(1)} %divide_bitcast_fusion.2, f32[128]{0:T(128)S(1)} %get-tuple-element.597, f32[16384]{0:T(1024)S(1)} %bitcast.176, f32[128]{0:T(128)S(1)} %get-tuple-element.598, ...), kind=kLoop, calls=%fused_computation.66.clone.1 | loop fusion | flops 25165440 | bytes 16845824 | tf_op jit(solution)/shard_map/while/body/eval_jaxpr/transpose(jvp())/reduce_sum | solution.py:29
  460.1 19.5 %fusion.218 = (f32[16384,128]{1,0:T(8,128)S(1)}, f32[16384,128]{1,0:T(8,128)S(1)}) fusion(bf16[128,128]{1,0:T(8,128)(2,1)S(1)} %get-tuple-element.599, f32[128]{0:T(128)S(1)} %get-tuple-element.598, f32[128]{0:T(128)S(1)} %get-tuple-element.597, f32[16384]{0:T(1024)S(1)} %bitcast.173), kind=kOutput, calls=%fused_computation.69.clone.1 | convolution fusion | flops 679477248 | bytes 16876544 | tf_op jit(solution)/shard_map/while/body/eval_jaxpr/dot_general | solution.py:58
  480.4 4.3 add_convert_fusion.9
  492.2 7.4 %fusion.222 = (f32[128]{0:T(128)S(1)}, f32[128]{0:T(128)S(1)}, f32[128]{0:T(128)S(1)}) fusion(f32[16384,128]{1,0:T(8,128)S(1)} %get-tuple-element.529, f32[128]{0:T(128)S(1)} %divide_bitcast_fusion.2, f32[128]{0:T(128)S(1)} %get-tuple-element.597, f32[16384]{0:T(1024)S(1)} %bitcast.176, f32[128]{0:T(128)S(1)} %get-tuple-element.598, ...), kind=kLoop, calls=%fused_computation.66.clone.1 | loop fusion | flops 25165440 | bytes 16845824 | tf_op jit(solution)/shard_map/while/body/eval_jaxpr/transpose(jvp())/reduce_sum | solution.py:29
  501.3 19.5 %fusion.218 = (f32[16384,128]{1,0:T(8,128)S(1)}, f32[16384,128]{1,0:T(8,128)S(1)}) fusion(bf16[128,128]{1,0:T(8,128)(2,1)S(1)} %get-tuple-element.599, f32[128]{0:T(128)S(1)} %get-tuple-element.598, f32[128]{0:T(128)S(1)} %get-tuple-element.597, f32[16384]{0:T(1024)S(1)} %bitcast.173), kind=kOutput, calls=%fused_computation.69.clone.1 | convolution fusion | flops 679477248 | bytes 16876544 | tf_op jit(solution)/shard_map/while/body/eval_jaxpr/dot_general | solution.py:58
  533.4 7.4 %fusion.222 = (f32[128]{0:T(128)S(1)}, f32[128]{0:T(128)S(1)}, f32[128]{0:T(128)S(1)}) fusion(f32[16384,128]{1,0:T(8,128)S(1)} %get-tuple-element.529, f32[128]{0:T(128)S(1)} %divide_bitcast_fusion.2, f32[128]{0:T(128)S(1)} %get-tuple-element.597, f32[16384]{0:T(1024)S(1)} %bitcast.176, f32[128]{0:T(128)S(1)} %get-tuple-element.598, ...), kind=kLoop, calls=%fused_computation.66.clone.1 | loop fusion | flops 25165440 | bytes 16845824 | tf_op jit(solution)/shard_map/while/body/eval_jaxpr/transpose(jvp())/reduce_sum | solution.py:29
  550.8 21.7 %all-reduce.1 = (bf16[32,8]{0,1:T(8,128)(2,1)S(1)}, bf16[32,8]{0,1:T(8,128)(2,1)S(1)}, bf16[128,8]{0,1:T(8,128)(2,1)S(1)}) all-reduce(bf16[32,8]{0,1:T(8,128)(2,1)S(1)} %fusion.122, bf16[32,8]{0,1:T(8,128)(2,1)S(1)} %fusion.123, bf16[128,8]{0,1:T(8,128)(2,1)S(1)} %convert_element_type.292), channel_id=1, replica_groups=mesh['dp'=8,'tensor'=4] {'dp'}, use_global_device_ids=true, to_apply=%region_34.35 | all-reduce | flops 1536 | bytes 6144 | tf_op jit(solution)/shard_map/psum | solution.py:303
  587.6 37.3 %all-reduce = (f32[768]{0:T(1024)}, f32[768]{0:T(1024)}, f32[768]{0:T(1024)}, f32[768]{0:T(1024)}, f32[128]{0:T(128)}, /*index=5*/f32[128]{0:T(128)}) all-reduce(f32[768]{0:T(1024)S(1)} %get-tuple-element.320, f32[768]{0:T(1024)S(1)} %get-tuple-element.319, ...), channel_id=1, replica_groups=mesh['dp'=8,'tensor'=4] {'dp','tensor'}, use_global_device_ids=true, to_apply=%region_25.26 | all-reduce | flops 3328 | bytes 26624 | tf_op jit(solution)/shard_map/psum | solution.py:307
  632.9 60.3 %all-reduce.14.cloned.1.call-done = f32[128,128]{1,0:T(8,128)} async-done(((f32[128,128]{1,0:T(8,128)}), f32[128,128]{1,0:T(8,128)}) %all-reduce.14.cloned.1.call-update) | async-done | bytes 65552 | tf_op jit(solution)/shard_map/psum | solution.py:307
  (359 shorter events, 198.9 us)
Async XLA Ops:
  7.2 245.3 %all-reduce.10.cloned.1.call-start = ((), (), s32[]{:S(2)}) async-start(), calls=%async_computation | async-start | bytes 3145728 | tf_op jit(solution)/shard_map/psum | solution.py:233
  160.1 38.8 %copy-start.26 = (bf16[16,64,8,24]{1,0,3,2:T(8,128)(2,1)}, bf16[16,64,8,24]{1,0,3,2:T(8,128)(2,1)S(1)}, u32[]{:S(2)}) copy-start(bf16[16,64,8,24]{1,0,3,2:T(8,128)(2,1)S(1)} %convert_element_type.239) | copy-start | bytes 1179652
  163.7 26.0 %copy-start.18 = (bf16[16,64,8,24]{1,0,3,2:T(8,128)(2,1)}, bf16[16,64,8,24]{1,0,3,2:T(8,128)(2,1)S(1)}, u32[]{:S(2)}) copy-start(bf16[16,64,8,24]{1,0,3,2:T(8,128)(2,1)S(1)} %convert_element_type.242) | copy-start | bytes 1179652
  206.8 105.7 %all-reduce.12.cloned.1.call-start = ((), (), s32[]{:S(2)}) async-start(), calls=%async_computation.1 | async-start | bytes 3145728 | tf_op jit(solution)/shard_map/psum | solution.py:247
  210.0 46.9 %copy-start.64 = (f32[256]{0:T(256)}, f32[256]{0:T(256)S(1)}, u32[]{:S(2)}) copy-start(f32[256]{0:T(256)S(1)} %broadcast_multiply_fusion.5) | copy-start | bytes 3076
  211.9 45.0 %copy-start.45 = (f32[768]{0:T(1024)S(1)}, f32[768]{0:T(1024)}, u32[]{:S(2)}) copy-start(f32[768]{0:T(1024)} %param.33) | copy-start | bytes 9220
  211.9 45.0 %copy-start.70 = (f32[768]{0:T(1024)S(1)}, f32[768]{0:T(1024)}, u32[]{:S(2)}) copy-start(f32[768]{0:T(1024)} %param.34) | copy-start | bytes 9220
  265.8 9.8 %copy-start.66 = (f32[256]{0:T(256)}, f32[256]{0:T(256)S(1)}, u32[]{:S(2)}) copy-start(f32[256]{0:T(256)S(1)} %broadcast_multiply_fusion.4) | copy-start | bytes 3076
  269.4 308.0 %all-reduce.18.cloned.1.call-start = ((), (), s32[]{:S(2)}) async-start(), calls=%async_computation.4 | async-start | bytes 6291456 | tf_op jit(solution)/shard_map/psum | solution.py:239
  334.4 10.3 %copy-start.28 = (bf16[16,64,8,24]{1,3,2,0:T(8,128)(2,1)S(1)}, bf16[16,64,8,24]{1,3,2,0:T(8,128)(2,1)}, u32[]{:S(2)}) copy-start(bf16[16,64,8,24]{1,3,2,0:T(8,128)(2,1)} %fusion.115) | copy-start | bytes 1179652
  339.8 11.4 %copy-start.85 = (f32[3]{0:T(128)S(1)}, f32[3]{0:T(128)}, u32[]{:S(2)}) copy-start(f32[3]{0:T(128)} %constant.348.clone) | copy-start | bytes 40
  354.0 271.0 %all-reduce.16.cloned.1.call-start = ((), (), s32[]{:S(2)}) async-start(), calls=%async_computation.3 | async-start | bytes 3538944 | tf_op jit(solution)/shard_map/psum | solution.py:299
  362.3 9.1 %copy-start.23 = (bf16[1024,192]{0,1:T(8,128)(2,1)S(1)}, bf16[1024,192]{0,1:T(8,128)(2,1)}, u32[]{:S(2)}) copy-start(bf16[1024,192]{0,1:T(8,128)(2,1)} %reshape.250) | copy-start | bytes 1179652
  376.5 316.8 %all-reduce.14.cloned.1.call-start = ((), (), s32[]{:S(2)}) async-start(), calls=%async_computation.2 | async-start | bytes 131072 | tf_op jit(solution)/shard_map/psum | solution.py:307
  376.5 165.1 %copy-start.17 = (bf16[16,64,64,8]{1,2,3,0:T(8,128)(2,1)S(1)}, bf16[16,64,64,8]{1,2,3,0:T(8,128)(2,1)}, u32[]{:S(2)}) copy-start(bf16[16,64,64,8]{1,2,3,0:T(8,128)(2,1)} %get-tuple-element.374) | copy-start | bytes 3145732
  376.6 20.7 %copy-start.83 = (f32[1,128]{1,0:T(1,128)}, f32[1,128]{1,0:T(1,128)S(1)}, u32[]{:S(2)}) copy-start(f32[1,128]{1,0:T(1,128)S(1)} %get-tuple-element.602) | copy-start | bytes 1540 | tf_op jit(solution)/shard_map/while
  377.7 19.5 %copy-start.22 = (bf16[4,16384,8]{1,2,0:T(8,128)(2,1)S(1)}, bf16[4,16384,8]{1,2,0:T(8,128)(2,1)}, u32[]{:S(2)}) copy-start(bf16[4,16384,8]{1,2,0:T(8,128)(2,1)} %get-tuple-element.600) | copy-start | bytes 3145732 | tf_op jit(solution)/shard_map/while
  409.8 8.0 %copy-start.84 = (f32[1,128]{1,0:T(1,128)S(1)}, f32[1,128]{1,0:T(1,128)}, u32[]{:S(2)}) copy-start(f32[1,128]{1,0:T(1,128)} %copy-done.83) | copy-start | bytes 1540 | tf_op jit(solution)/shard_map/while
  417.9 20.5 %copy-start.83 = (f32[1,128]{1,0:T(1,128)}, f32[1,128]{1,0:T(1,128)S(1)}, u32[]{:S(2)}) copy-start(f32[1,128]{1,0:T(1,128)S(1)} %get-tuple-element.602) | copy-start | bytes 1540 | tf_op jit(solution)/shard_map/while
  418.9 19.5 %copy-start.22 = (bf16[4,16384,8]{1,2,0:T(8,128)(2,1)S(1)}, bf16[4,16384,8]{1,2,0:T(8,128)(2,1)}, u32[]{:S(2)}) copy-start(bf16[4,16384,8]{1,2,0:T(8,128)(2,1)} %get-tuple-element.600) | copy-start | bytes 3145732 | tf_op jit(solution)/shard_map/while
  451.0 8.0 %copy-start.84 = (f32[1,128]{1,0:T(1,128)S(1)}, f32[1,128]{1,0:T(1,128)}, u32[]{:S(2)}) copy-start(f32[1,128]{1,0:T(1,128)} %copy-done.83) | copy-start | bytes 1540 | tf_op jit(solution)/shard_map/while
  459.0 20.5 %copy-start.83 = (f32[1,128]{1,0:T(1,128)}, f32[1,128]{1,0:T(1,128)S(1)}, u32[]{:S(2)}) copy-start(f32[1,128]{1,0:T(1,128)S(1)} %get-tuple-element.602) | copy-start | bytes 1540 | tf_op jit(solution)/shard_map/while
  460.1 19.5 %copy-start.22 = (bf16[4,16384,8]{1,2,0:T(8,128)(2,1)S(1)}, bf16[4,16384,8]{1,2,0:T(8,128)(2,1)}, u32[]{:S(2)}) copy-start(bf16[4,16384,8]{1,2,0:T(8,128)(2,1)} %get-tuple-element.600) | copy-start | bytes 3145732 | tf_op jit(solution)/shard_map/while
  492.2 8.0 %copy-start.84 = (f32[1,128]{1,0:T(1,128)S(1)}, f32[1,128]{1,0:T(1,128)}, u32[]{:S(2)}) copy-start(f32[1,128]{1,0:T(1,128)} %copy-done.83) | copy-start | bytes 1540 | tf_op jit(solution)/shard_map/while
  500.2 20.5 %copy-start.83 = (f32[1,128]{1,0:T(1,128)}, f32[1,128]{1,0:T(1,128)S(1)}, u32[]{:S(2)}) copy-start(f32[1,128]{1,0:T(1,128)S(1)} %get-tuple-element.602) | copy-start | bytes 1540 | tf_op jit(solution)/shard_map/while
  501.3 19.5 %copy-start.22 = (bf16[4,16384,8]{1,2,0:T(8,128)(2,1)S(1)}, bf16[4,16384,8]{1,2,0:T(8,128)(2,1)}, u32[]{:S(2)}) copy-start(bf16[4,16384,8]{1,2,0:T(8,128)(2,1)} %get-tuple-element.600) | copy-start | bytes 3145732 | tf_op jit(solution)/shard_map/while
  550.8 25.2 %copy-start.67 = (f32[256]{0:T(256)S(1)}, f32[256]{0:T(256)}, u32[]{:S(2)}) copy-start(f32[256]{0:T(256)} %copy-done.66) | copy-start | bytes 3076
  550.8 25.2 %copy-start.72 = (f32[256]{0:T(256)S(1)}, f32[256]{0:T(256)}, u32[]{:S(2)}) copy-start(f32[256]{0:T(256)} %add_rsqrt_fusion) | copy-start | bytes 3076
  550.8 26.6 %copy-start.3 = (bf16[1024,768]{1,0:T(8,128)(2,1)S(1)}, bf16[1024,768]{1,0:T(8,128)(2,1)}, u32[]{:S(2)}) copy-start(bf16[1024,768]{1,0:T(8,128)(2,1)} %param.26) | copy-start | bytes 4718596
  550.8 26.6 %copy-start.42 = (f32[1024]{0:T(1024)S(1)}, f32[1024]{0:T(1024)}, u32[]{:S(2)}) copy-start(f32[1024]{0:T(1024)} %copy-done.40) | copy-start | bytes 12292
  550.8 26.6 %copy-start.49 = (f32[768]{0:T(1024)S(1)}, f32[768]{0:T(1024)}, u32[]{:S(2)}) copy-start(f32[768]{0:T(1024)} %param.31) | copy-start | bytes 9220
  583.1 111.6 %copy-start.1 = (bf16[3,768,192]{1,2,0:T(8,128)(2,1)S(1)}, bf16[3,768,192]{1,2,0:T(8,128)(2,1)}, u32[]{:S(2)}) copy-start(bf16[3,768,192]{1,2,0:T(8,128)(2,1)} %param.27) | copy-start | bytes 2654212
  (81 other events, 310.2 us)
Sparse Core Ops, SparseCore 0:
  206.9 45.5 all-reduce.9
  269.5 42.9 all-reduce.11
  354.1 68.5 all-reduce.17
  427.0 93.9 all-reduce.15
  577.5 115.7 all-reduce.13
where the time goes:
time: 708 us; the launch traced here: 702 us
  matrix products  279 us (39%)
  waiting for transfers between devices  138 us (19%)
  local copies, waits for them, and re-layouts  115 us (16%)
  other arithmetic  94.6 us (13%)
  blocking collectives  59.1 us (8%)
  between operations  15.1 us (2%)
    dot_general x4, matrix products, one_block(): return jnp.dot(hidden, kernel_w2, preferred_element_type=jnp.float32)  84.6 us
    dot_general x4, matrix products, one_block(): inner = jnp.dot(basis_b, kernel_w1, preferred_element_type=jnp.float32)  77.8 us
    psum x1, waiting for transfers between devices, body(): lax.psum((grad_kw1, grad_cen, grad_wid, grad_g1, grad_b1, grad_g2, grad_b...  60.3 us
    dynamic_update_slice x8, local copies, waits for them, and re-layouts, kernel_geo(): result = lax.map(one_block, dist_rows.reshape(total // block, block))  44.1 us
    psum x1, waiting for transfers between devices, body(): lax.psum(attn_part.astype(jnp.bfloat16), 'tensor').astype(jnp.float32)  40.5 us
    psum x1, blocking collectives, body(): lax.psum((grad_kw1, grad_cen, grad_wid, grad_g1, grad_b1, grad_g2, grad_b...  37.3 us
    psum x1, waiting for transfers between devices, body(): lax.psum(two_part.astype(jnp.bfloat16), 'tensor').astype(jnp.float32)  36.9 us
    reduce_sum x4, other arithmetic, kernels(): offset = (place - centers) / widths  29.6 us
  transfers between devices with their start and end apart: 5, of which 3 were waited for; matrix products, arithmetic and copies ran while one was open for 32% of the time, Pallas kernels for 0%

commit v1 on v0

v1 whole, which is shorter than its diff:
```python
import math

import jax
import jax.numpy as jnp
from jax import lax
from jax.experimental import pallas as pl
from jax.experimental.pallas import tpu as pltpu
from jax.sharding import PartitionSpec as P

EPS = 1e-05
NEG = -1000000000.0
F32 = jnp.float32
BF16 = jnp.bfloat16
NN = (((1,), (0,)), ((), ()))
NT = (((1,), (1,)), ((), ()))
TN = (((0,), (0,)), ((), ()))
CHUNKS = 2
SPD = 32
DIST = 128


def dot(left, right, dims):
    return lax.dot_general(left, right, dims, preferred_element_type=F32)


def cdf(values):
    return 0.5 * (1.0 + lax.erf(values * math.sqrt(0.5)))


def gelu_slope(values, phi):
    return phi + values * jnp.exp(-0.5 * values * values) * (1.0 / math.sqrt(2.0 * math.pi))


def normed(values):
    center = values - jnp.mean(values, axis=-1, keepdims=True)
    rstd = lax.rsqrt(jnp.mean(center * center, axis=-1, keepdims=True) + EPS)
    return center * rstd, rstd


def norm_back(hat, rstd, gain, grad):
    scaled = grad * gain
    mean_one = jnp.mean(scaled, axis=-1, keepdims=True)
    mean_two = jnp.mean(scaled * hat, axis=-1, keepdims=True)
    return rstd * (scaled - mean_one - hat * mean_two)


def basis_of(centers, widths):
    place = lax.broadcasted_iota(jnp.int32, (DIST, 1), 0).astype(F32) * (8.0 / DIST)
    offset = (place - centers) / widths
    return offset, jnp.exp(-0.5 * offset * offset) / widths


def table_kernel(w2t_ref, w1_ref, cen_ref, wid_ref, geo_ref):
    phi = basis_of(cen_ref[...], wid_ref[...])[1].astype(BF16)
    z = dot(phi, w1_ref[...], NN)
    gz = (z * cdf(z)).astype(BF16)
    geo_ref[...] = dot(w2t_ref[...].astype(BF16), gz, NT)


def half_lanes(rows):
    return lax.broadcasted_iota(jnp.int32, (rows, 128), 1) >= 64


def splits(block, half_cols, col):
    zero = jnp.zeros_like(block)
    return jnp.concatenate(
        [jnp.where(col < half_cols, block, zero), jnp.where(col >= half_cols, block, zero)], 0
    )


def pair_masks(col, head_dim, pairs):
    head = col // head_dim
    return [jnp.logical_or(head == p, head == p + pairs) for p in range(pairs)]


def pair_stack(block, masks):
    zero = jnp.zeros_like(block)
    return jnp.concatenate([jnp.where(mask, block, zero) for mask in masks], 0)


def lookup(row, index):
    wide = jnp.broadcast_to(row, index.shape)
    return jnp.take_along_axis(wide, index, axis=1, mode="promise_in_bounds")


def forward_kernel(dims, *refs):
    mols, columns, pairs, head_dim = dims
    (where_ref, count_ref, mode_ref, x_ref, gain_ref, bias_ref, wq0, wq1, wo0, wo1) = refs[:10]
    (flat_ref, geo_ref, code_ref, part_ref, h1_ref, qkv_ref, o_ref, pt_ref) = refs[10:]
    base = where_ref[1]
    scale = 1.0 / math.sqrt(head_dim)
    hat = normed(x_ref[...].astype(F32))[0]
    h1 = (hat * gain_ref[...] + bias_ref[...]).astype(BF16)
    h1_ref[...] = h1
    for g, wq in enumerate((wq0, wq1)):
        for k in range(3):
            out = dot(h1, wq[k], NN)
            if k == 0:
                out = out * scale
            qkv_ref[3 * g + k] = out.astype(BF16)
    col = lax.broadcasted_iota(jnp.int32, (64, columns), 1)
    masks = pair_masks(col, head_dim, pairs)
    half_cols = pairs * head_dim
    half = half_lanes(64)
    row_id = lax.broadcasted_iota(jnp.int32, (64, 128), 0)

    def one(m, carry):
        rows = pl.ds(pl.multiple_of(m * 64, 64), 64)
        code = code_ref[m]
        spd_id = (code & 31) + jnp.where(half, 32, 0)
        edge_id = ((code >> 5) & 31) + jnp.where(half, 96, 64)
        dist_id = code >> 10
        keep = row_id < count_ref[base + m]
        mode = mode_ref[base + m]
        two = jnp.where(mode != 1, 1.0, 0.0).astype(F32)
        three = jnp.where(mode != 0, 1.0, 0.0).astype(F32)
        for g in range(2):
            query, keyset, values = (qkv_ref[3 * g + k, rows, :] for k in range(3))
            scores = dot(pair_stack(keyset, masks), splits(query, half_cols, col), NT)
            probs = []
            for p in range(pairs):
                flat = flat_ref[g * pairs + p : g * pairs + p + 1, :] * two
                low = geo_ref[2 * pairs * g + p : 2 * pairs * g + p + 1, :] * three
                high = geo_ref[2 * pairs * g + pairs + p : 2 * pairs * g + pairs + p + 1, :] * three
                bias = lookup(flat, spd_id) + lookup(flat, edge_id)
                bias = bias + jnp.where(half, lookup(high, dist_id), lookup(low, dist_id))
                part = jnp.where(keep, scores[p * 64 : p * 64 + 64] + bias, NEG)
                expos = jnp.exp(part - jnp.max(part, axis=0, keepdims=True))
                total = jnp.sum(expos, axis=0, keepdims=True)
                probs.append((expos / total).astype(BF16))
            probs = jnp.concatenate(probs, 0)
            pt_ref[m, g] = probs
            mixed = dot(probs, pair_stack(values, masks), TN)
            o_ref[g, rows, :] = jnp.where(col < half_cols, mixed[:64], mixed[64:]).astype(BF16)
        return carry

    lax.fori_loop(0, mols, one, 0)
    part_ref[...] = (dot(o_ref[0], wo0[...], NN) + dot(o_ref[1], wo1[...], NN)).astype(BF16)


def ffn_kernel(where_ref, *refs):
    (x_ref, pa_ref, pb_ref, c_ref, gain_ref, bias_ref, w10, w11, w20, w21) = refs[:10]
    (y1_ref, h2_ref, act_ref, ffn_ref, two_ref) = refs[10:]
    y1 = x_ref[...].astype(F32) + (pa_ref[...].astype(F32) + pb_ref[...].astype(F32))
    y1_ref[...] = y1
    h2 = (normed(y1)[0] * gain_ref[...] + bias_ref[...]).astype(BF16)
    h2_ref[...] = h2
    cot = c_ref[...]
    ffn, two = None, None
    for g, (w1, w2) in enumerate(((w10, w20), (w11, w21))):
        u = dot(h2, w1[...], NN)
        phi = cdf(u)
        act = (u * phi).astype(BF16)
        du = (dot(cot, w2[...], NT) * gelu_slope(u, phi)).astype(BF16)
        act_ref[2 * g] = act
        act_ref[2 * g + 1] = du
        one_ffn, one_two = dot(act, w2[...], NN), dot(du, w1[...], NT)
        ffn = one_ffn if ffn is None else ffn + one_ffn
        two = one_two if two is None else two + one_two
    ffn_ref[...] = ffn.astype(BF16)
    two_ref[...] = two.astype(BF16)


def ffn_grad_kernel(where_ref, *refs):
    chunks = (len(refs) - 1) // 3
    c_refs, h_refs, a_refs, out_ref = (
        refs[:chunks],
        refs[chunks : 2 * chunks],
        refs[2 * chunks : 3 * chunks],
        refs[-1],
    )
    for g in range(2):
        one, two = None, None
        for c_ref, h_ref, a_ref in zip(c_refs, h_refs, a_refs):
            more_one, more_two = dot(a_ref[2 * g + 1], h_ref[...], TN), dot(a_ref[2 * g], c_ref[...], TN)
            one = more_one if one is None else one + more_one
            two = more_two if two is None else two + more_two
        out_ref[g, 0] = one.astype(BF16)
        out_ref[g, 1] = two.astype(BF16)


def backward_kernel(dims, *refs):
    mols, columns, pairs, head_dim, share = dims
    (where_ref, mode_ref, x_ref, c_ref, y1_ref, ta_ref, tb_ref, g1_ref, g2_ref) = refs[:9]
    (wq0, wq1, wo0, wo1, code_ref, qkv_ref, pt_ref) = refs[9:16]
    (dy1_ref, gb_ref, dqkv_ref, one_ref, sums_ref, tabs_ref, do_ref, ds_ref, lhs_ref) = refs[16:]
    base = where_ref[1]
    scale = 1.0 / math.sqrt(head_dim)
    hat, rstd = normed(y1_ref[...])
    dh2 = ta_ref[...].astype(F32) + tb_ref[...].astype(F32)
    dy1 = c_ref[...].astype(F32) + norm_back(hat, rstd, g2_ref[...], dh2)
    dy1_ref[...] = dy1
    gain_two = jnp.sum(dh2 * hat, axis=0, keepdims=True) * share
    bias_two = jnp.sum(dh2, axis=0, keepdims=True) * share
    gb = dy1.astype(BF16)
    gb_ref[...] = gb
    for g, wo in enumerate((wo0, wo1)):
        do_ref[g] = dot(gb, wo[...], NT).astype(BF16)
    col = lax.broadcasted_iota(jnp.int32, (64, columns), 1)
    masks = pair_masks(col, head_dim, pairs)
    half_cols = pairs * head_dim
    heads = 4 * pairs
    low_half = jnp.logical_not(half_lanes(2 * pairs))
    low_32 = jnp.logical_not(half_lanes(32))
    row_128 = lax.broadcasted_iota(jnp.int32, (128, 128), 0)
    row_32 = lax.broadcasted_iota(jnp.int32, (32, 128), 0)
    tabs_ref[...] = jnp.zeros_like(tabs_ref)

    def own_pair(block):
        out = jnp.where(masks[0], block[:64], 0.0)
        for p in range(1, pairs):
            out = jnp.where(masks[p], block[p * 64 : p * 64 + 64], out)
        return out

    def one(m, carry):
        rows = pl.ds(pl.multiple_of(m * 64, 64), 64)
        for g in range(2):
            query, keyset, values = (qkv_ref[3 * g + k, rows, :] for k in range(3))
            grad = splits(do_ref[g, rows, :], half_cols, col)
            probs = pt_ref[m, g]
            dqkv_ref[3 * g + 2, rows, :] = own_pair(dot(probs, grad, NN)).astype(BF16)
            dprob = dot(pair_stack(values, masks), grad, NT)
            wide = probs.astype(F32)
            pieces = []
            for p in range(pairs):
                part = wide[p * 64 : p * 64 + 64]
                dp = dprob[p * 64 : p * 64 + 64]
                ds = part * (dp - jnp.sum(part * dp, axis=0, keepdims=True))
                pieces.append(ds.astype(BF16))
                ds_ref[pl.ds((g * pairs + p) * 64, 64), :] = ds
            ds = jnp.concatenate(pieces, 0)
            dq = dot(ds, pair_stack(keyset, masks), TN)
            dq = jnp.where(col < half_cols, dq[:64], dq[64:]) * scale
            dqkv_ref[3 * g, rows, :] = dq.astype(BF16)
            dk = own_pair(dot(ds, splits(query, half_cols, col), NN))
            dqkv_ref[3 * g + 1, rows, :] = dk.astype(BF16)
        code = code_ref[m]
        code = jnp.where(low_32, code[:32], code[32:])
        mode = mode_ref[base + m]
        spd_id = jnp.where(mode != 1, code & 31, -1)
        edge_id = jnp.where(mode != 1, (code >> 5) & 31, -1)
        dist_id = jnp.where(mode != 0, code >> 10, -1)
        hots = []
        for j in range(32):
            first = ds_ref[pl.ds(j, 2 * pairs, stride=64), :]
            second = ds_ref[pl.ds(j + 32, 2 * pairs, stride=64), :]
            left = jnp.where(low_half, first, pltpu.roll(second, 64, 1))
            right = jnp.where(low_half, pltpu.roll(first, 64, 1), second)
            lhs_ref[:, j * 128 : j * 128 + 128] = jnp.concatenate([left, right], 0).astype(BF16)
            hots.append(
                jnp.concatenate(
                    [
                        jnp.where(row_128 == dist_id[j : j + 1], 1.0, 0.0),
                        jnp.where(row_32 == spd_id[j : j + 1], 1.0, 0.0),
                        jnp.where(row_32 == edge_id[j : j + 1], 1.0, 0.0),
                    ],
                    0,
                ).astype(BF16)
            )
        total = None
        for j in range(0, 32, 2):
            hot = jnp.concatenate(hots[j : j + 2], 1)
            more = dot(lhs_ref[:, j * 128 : j * 128 + 256], hot, NT)
            total = more if total is None else total + more
        tabs_ref[...] += total
        return carry

    lax.fori_loop(0, mols, one, 0)
    part = None
    for g, wq in enumerate((wq0, wq1)):
        for k in range(3):
            more = dot(dqkv_ref[3 * g + k], wq[k], NT)
            part = more if part is None else part + more
    one_ref[...] = part.astype(BF16)
    hat = normed(x_ref[...].astype(F32))[0]
    sums_ref[...] = jnp.concatenate(
        [
            jnp.sum(part * hat, axis=0, keepdims=True),
            jnp.sum(part, axis=0, keepdims=True),
            gain_two,
            bias_two,
        ],
        0,
    )


def proj_grad_kernel(*refs):
    chunks = (len(refs) - 2) // 4
    h_refs, d_refs, o_refs, g_refs = (refs[i * chunks : (i + 1) * chunks] for i in range(4))
    qkv_ref, out_ref = refs[-2:]
    for g in range(2):
        for k in range(4):
            total = None
            for h_ref, d_ref, o_ref, g_ref in zip(h_refs, d_refs, o_refs, g_refs):
                if k < 3:
                    more = dot(d_ref[3 * g + k], h_ref[...], TN)
                else:
                    more = dot(o_ref[g], g_ref[...], TN)
                total = more if total is None else total + more
            if k < 3:
                qkv_ref[g, k] = total.astype(BF16)
            else:
                out_ref[g] = total.astype(BF16)


def finish_kernel(where_ref, *refs):
    x_ref, dy1_ref, a_ref, b_ref, gain_ref, out_ref = refs
    hat, rstd = normed(x_ref[...].astype(F32))
    grad = a_ref[...].astype(F32) + b_ref[...].astype(F32)
    out_ref[...] = (dy1_ref[...] + norm_back(hat, rstd, gain_ref[...], grad)).astype(BF16)


def kernel_net_kernel(geo_ref, w2_ref, w1_ref, cen_ref, wid_ref, g1_ref, g2_ref, cw_ref):
    wid = wid_ref[...]
    offset, phi = basis_of(cen_ref[...], wid)
    phi_b = phi.astype(BF16)
    z = dot(phi_b, w1_ref[...], NN)
    cum = cdf(z)
    gz = z * cum
    high = lax.Precision.HIGHEST
    dgeo = geo_ref[...]
    g2_ref[...] = lax.dot_general(dgeo, gz.astype(BF16).astype(F32), NN, precision=high)
    dgz = lax.dot_general(dgeo, w2_ref[...], TN, precision=high)
    dz = dgz * gelu_slope(z, cum)
    g1_ref[...] = lax.dot_general(phi_b.astype(F32), dz, TN, precision=high)
    dphi = lax.dot_general(dz, w1_ref[...].astype(F32), NT, precision=high)
    scaled = dphi * phi / wid
    cw_ref[...] = jnp.concatenate(
        [
            jnp.sum(scaled * offset, axis=0, keepdims=True),
            jnp.sum(scaled * (offset * offset - 1.0), axis=0, keepdims=True),
        ],
        0,
    )


def shape(dims, dtype=BF16):
    return jax.ShapeDtypeStruct(dims, dtype)


def whole(dims):
    return pl.BlockSpec(dims, lambda *_: (0,) * len(dims))


def flips(count, bit):
    return [(i, i ^ (1 << bit)) for i in range(count)]


def bits_of(count):
    return range(count.bit_length() - 1)


def body(
    hidden_in,
    w_qkv,
    w_out,
    w_ff1,
    w_ff2,
    ln1_gain,
    ln1_bias,
    ln2_gain,
    ln2_bias,
    spd_table,
    edge_table,
    kernel_w1,
    kernel_w2,
    centers,
    widths,
    atom_count,
    mol_mode,
    spd_bucket,
    edge_type,
    dist_bucket,
    cotangent,
):
    tokens, width = hidden_in.shape
    mols = spd_bucket.shape[0]
    columns = w_qkv.shape[2]
    heads = spd_table.shape[1]
    pairs = heads // 2
    head_dim = columns // heads
    tensor, data = lax.axis_size("tensor"), lax.axis_size("dp")
    t_index, d_index = lax.axis_index("tensor"), lax.axis_index("dp")
    core = t_index % 2
    my_mols = mols // 2
    n_mols = my_mols // CHUNKS
    rows = n_mols * 64

    def other(array):
        return lax.ppermute(array, "tensor", flips(tensor, 0))

    def across(array):
        for bit in list(bits_of(tensor))[1:]:
            sent = lax.ppermute(array, "tensor", flips(tensor, bit))
            if bit < tensor.bit_length() - 2:
                array = (array.astype(F32) + sent.astype(F32)).astype(BF16)
        return array, sent

    def row(vector):
        return vector.reshape(1, -1)

    gain1, bias1, gain2, bias2 = (row(v) for v in (ln1_gain, ln1_bias, ln2_gain, ln2_bias))
    cen, wid = row(centers), row(widths)
    spd_t, edge_t = spd_table.T, edge_table.T
    flat = jnp.concatenate([spd_t[:pairs], spd_t[pairs:], edge_t[:pairs], edge_t[pairs:]], 1)
    small = jnp.concatenate([flat, kernel_w2.T.astype(F32)], 0)
    small_other = other(small)
    wq_other = other(w_qkv)
    wo_other = other(w_out)
    w1_other = other(w_ff1)
    w2_other = other(w_ff2)
    w2t = jnp.concatenate([small[pairs:], small_other[pairs:]], 0)
    flat = jnp.concatenate([flat, small_other[:pairs]], 0)
    geo = pl.pallas_call(
        table_kernel, out_shape=shape((2 * heads, DIST), F32), name="bucket_table"
    )(w2t, kernel_w1, cen, wid)

    def mine(array):
        return lax.dynamic_slice_in_dim(array, core * my_mols, my_mols, 0)

    code = mine(spd_bucket) | (mine(edge_type) << 5) | (mine(dist_bucket) << 10)
    code = jnp.swapaxes(code, 1, 2)
    code = jnp.concatenate([code, code], 2)

    def place(chunk):
        return jnp.stack([core * CHUNKS + chunk, core * my_mols + chunk * n_mols]).astype(jnp.int32)

    places = [place(chunk) for chunk in range(CHUNKS)]
    row_block = pl.BlockSpec((rows, width), lambda i, at, *_: (at[0], 0))
    act_block = whole((rows, width))
    vec = whole((1, width))
    wq_spec, wo_spec = whole(w_qkv.shape), whole(w_out.shape)
    w1_spec, w2_spec = whole(w_ff1.shape), whole(w_ff2.shape)
    qkv_spec, o_spec = whole((6, rows, columns)), whole((2, rows, columns))
    pt_spec = whole((n_mols, 2, pairs * 64, 128))

    def code_spec(chunk):
        return pl.BlockSpec((n_mols, 64, 128), lambda i, *_: (chunk, 0, 0))

    def call(kernel, scalars, ins, outs, shapes, name, scratch=()):
        spec = pltpu.PrefetchScalarGridSpec(
            num_scalar_prefetch=len(scalars), grid=(1,), in_specs=ins, out_specs=outs, scratch_shapes=list(scratch)
        )
        return pl.pallas_call(kernel, grid_spec=spec, out_shape=shapes, name=name)

    dims = (n_mols, columns, pairs, head_dim)
    parts, h1s, qkvs, os_, pts, crossed = [], [], [], [], [], []
    for chunk in range(CHUNKS):
        scalars = (places[chunk], atom_count, mol_mode)
        part, h1, qkv, mixed, probs = call(
            lambda *refs: forward_kernel(dims, *refs),
            scalars,
            [row_block, vec, vec, wq_spec, wq_spec, wo_spec, wo_spec]
            + [whole(flat.shape), whole(geo.shape), code_spec(chunk)],
            [act_block, act_block, qkv_spec, o_spec, pt_spec],
            [
                shape((rows, width)),
                shape((rows, width)),
                shape((6, rows, columns)),
                shape((2, rows, columns)),
                shape((n_mols, 2, pairs * 64, 128)),
            ],
            "attend",
        )(*scalars, hidden_in, gain1, bias1, w_qkv, wq_other, w_out, wo_other, flat, geo, code)
        h1s.append(h1), qkvs.append(qkv), os_.append(mixed), pts.append(probs)
        crossed.append(across(part))

    y1s, h2s, acts, ffns, twos = [], [], [], [], []
    for chunk in range(CHUNKS):
        y1, h2, act, ffn, two = call(
            ffn_kernel,
            (places[chunk],),
            [row_block, act_block, act_block, row_block, vec, vec, w1_spec, w1_spec, w2_spec, w2_spec],
            [act_block, act_block, whole((4, rows, columns)), act_block, act_block],
            [
                shape((rows, width), F32),
                shape((rows, width)),
                shape((4, rows, columns)),
                shape((rows, width)),
                shape((rows, width)),
            ],
            "ffn",
        )(places[chunk], hidden_in, *crossed[chunk], cotangent, gain2, bias2, w_ff1, w1_other, w_ff2, w2_other)
        y1s.append(y1), h2s.append(h2), acts.append(act), ffns.append(ffn)
        twos.append(across(two))

    c_block = pl.BlockSpec((rows, width), lambda i, at, *_: (at[0], 0))
    c_specs = [
        pl.BlockSpec((rows, width), lambda i, at, chunk=chunk: (at[0] + chunk, 0)) for chunk in range(CHUNKS)
    ]
    ff_grads = call(
        ffn_grad_kernel,
        (places[0],),
        c_specs + [act_block] * CHUNKS + [whole((4, rows, columns))] * CHUNKS,
        [whole((2, 2, columns, width))],
        [shape((2, 2, columns, width))],
        "ffn_grad",
    )(places[0], *([cotangent] * CHUNKS), *h2s, *acts)[0]

    dims = (n_mols, columns, pairs, head_dim, 2.0 / tensor)
    dy1s, gbs, dqkvs, ones, sums, tabs = [], [], [], [], None, None
    for chunk in range(CHUNKS):
        dy1, gb, dqkv, one, some, tab = call(
            lambda *refs: backward_kernel(dims, *refs),
            (places[chunk], mol_mode),
            [row_block, row_block, act_block, act_block, act_block, vec, vec]
            + [wq_spec, wq_spec, wo_spec, wo_spec, code_spec(chunk), qkv_spec, pt_spec],
            [act_block, act_block, qkv_spec, act_block, whole((4, width)), whole((2 * heads, 192))],
            [
                shape((rows, width), F32),
                shape((rows, width)),
                shape((6, rows, columns)),
                shape((rows, width)),
                shape((4, width), F32),
                shape((2 * heads, 192), F32),
            ],
            "attend_back",
            [
                pltpu.VMEM((2, rows, columns), BF16),
                pltpu.VMEM((2 * pairs * 64, 128), F32),
                pltpu.VMEM((2 * heads, 32 * 128), BF16),
            ],
        )(
            places[chunk], mol_mode, hidden_in, cotangent, y1s[chunk], *twos[chunk], gain1, gain2,
            w_qkv, wq_other, w_out, wo_other, code, qkvs[chunk], pts[chunk],
        )
        dy1s.append(dy1), gbs.append(gb), dqkvs.append(dqkv)
        ones.append(across(one))
        sums = some if sums is None else sums + some
        tabs = tab if tabs is None else tabs + tab

    qkv_grads, out_grads = pl.pallas_call(
        proj_grad_kernel,
        out_shape=[shape((2, 3, columns, width)), shape((2, columns, width))],
        name="proj_grad",
    )(*h1s, *dqkvs, *os_, *gbs)

    def reduced(grads):
        grads = grads.reshape(2, -1, width)
        got = other(grads[1])
        array = (grads[0].astype(F32) + got.astype(F32)).astype(BF16)
        for bit in bits_of(data):
            size = array.shape[0] // 2
            side = (d_index >> bit) & 1
            sent = lax.dynamic_slice_in_dim(array, (1 - side) * size, size, 0)
            kept = lax.dynamic_slice_in_dim(array, side * size, size, 0)
            got = lax.ppermute(sent, "dp", flips(data, bit))
            array = (kept.astype(F32) + got.astype(F32)).astype(BF16)
        for bit in reversed(bits_of(data)):
            got = lax.ppermute(array, "dp", flips(data, bit))
            side = (d_index >> bit) & 1
            array = jnp.where(
                side == 0, jnp.concatenate([array, got], 0), jnp.concatenate([got, array], 0)
            )
        return array.reshape(-1, columns, width).astype(F32)

    ff_sum = reduced(ff_grads)
    out_sum = reduced(out_grads)
    qkv_sum = reduced(qkv_grads)

    table = jnp.zeros((heads * tensor, 192), F32)
    table = lax.dynamic_update_slice_in_dim(table, heads_of(tabs, 0, heads, pairs), t_index * heads, 0)
    table = lax.dynamic_update_slice_in_dim(table, heads_of(tabs, 1, heads, pairs), (t_index ^ 1) * heads, 0)
    w2_full = jnp.zeros((heads * tensor, 128), F32)
    w2_full = lax.dynamic_update_slice_in_dim(w2_full, small[pairs:], t_index * heads, 0)
    for bit in bits_of(tensor):
        w2_full = w2_full + lax.ppermute(w2_full, "tensor", flips(tensor, bit))
    packed = jnp.concatenate([table, sums.reshape(-1, 192)], 0)
    for bit in bits_of(tensor):
        packed = packed + lax.ppermute(packed, "tensor", flips(tensor, bit))
    for bit in bits_of(data):
        packed = packed + lax.ppermute(packed, "dp", flips(data, bit))
    table, sums = packed[: heads * tensor], packed[heads * tensor :].reshape(4, width)
    grad_kw1, grad_kw2, grad_cw = pl.pallas_call(
        kernel_net_kernel,
        out_shape=[shape((128, 128), F32), shape((heads * tensor, 128), F32), shape((2, 128), F32)],
        name="kernel_net",
    )(table[:, :DIST], w2_full, kernel_w1, cen, wid)
    own = lax.dynamic_slice_in_dim(table, t_index * heads, heads, 0).T
    grad_kw2 = lax.dynamic_slice_in_dim(grad_kw2, t_index * heads, heads, 0).T

    finals, outs = [], []
    for chunk in range(CHUNKS):
        finals.append(
            call(
                finish_kernel,
                (places[chunk],),
                [row_block, act_block, act_block, act_block, vec],
                act_block,
                shape((rows, width)),
                "finish",
            )(places[chunk], hidden_in, dy1s[chunk], *ones[chunk], gain1)
        )
        ffn_a, ffn_b = across(ffns[chunk])
        outs.append((y1s[chunk] + (ffn_a.astype(F32) + ffn_b.astype(F32))).astype(BF16))

    def joined(pieces):
        piece = jnp.concatenate(pieces, 0)
        got = other(piece)
        return jnp.where(core == 0, jnp.concatenate([piece, got], 0), jnp.concatenate([got, piece], 0))

    return (
        joined(outs),
        joined(finals),
        jnp.swapaxes(qkv_sum, 1, 2),
        out_sum[0],
        ff_sum[0].T,
        ff_sum[1],
        sums[0],
        sums[1],
        sums[2],
        sums[3],
        own[DIST : DIST + SPD],
        own[DIST + SPD :],
        grad_kw1,
        grad_kw2,
        grad_cw[0],
        grad_cw[1],
    )


def heads_of(tabs, group, heads, pairs):
    view = tabs.reshape(2, 2, pairs, tabs.shape[1])
    return view[:, group].reshape(heads, tabs.shape[1])


def solution(mesh):
    in_specs = (
        P("dp", None),
        P(None, None, "tensor"),
        P("tensor", None),
        P(None, "tensor"),
        P("tensor", None),
        P(),
        P(),
        P(),
        P(),
        P(None, "tensor"),
        P(None, "tensor"),
        P(),
        P(None, "tensor"),
        P(),
        P(),
        P("dp"),
        P("dp"),
        P("dp", None, None),
        P("dp", None, None),
        P("dp", None, None),
        P("dp", None),
    )
    out_specs = (
        P("dp", None),
        P("dp", None),
        P(None, None, "tensor"),
        P("tensor", None),
        P(None, "tensor"),
        P("tensor", None),
        P(),
        P(),
        P(),
        P(),
        P(None, "tensor"),
        P(None, "tensor"),
        P(),
        P(None, "tensor"),
        P(),
        P(),
    )
    return jax.shard_map(body, mesh=mesh, in_specs=in_specs, out_specs=out_specs, check_vma=False)
```

time: 708 us -> 222 us (0.31)
  matrix products: 279 us -> 0 us
  waiting for transfers between devices: 138 us -> 47.2 us
  local copies, waits for them, and re-layouts: 115 us -> 28.8 us
  Pallas kernels: 0 us -> 71.9 us
  other arithmetic: 94.6 us -> 24.5 us
  blocking collectives: 59.1 us -> 0 us
  starting transfers between devices: 0.2 us -> 47.7 us
  between operations: 15.1 us -> 1.15 us
    dot_general x45 -> x0, matrix products: 276 us -> none  [the longest x4 84.6 us: one_block(): return jnp.dot(hidden, kernel_w2, preferred_element_type=jnp.float32)]
    psum x5 -> x0, waiting for transfers between devices: 138 us -> none  [the longest x1 60.3 us: body(): lax.psum((grad_kw1, grad_cen, grad_wid, grad_g1, grad_b1, grad_g2, grad_b...]
    pallas_call x0 -> x12, Pallas kernels: none -> 71.9 us  [the longest x2 24.2 us: body(): call(lambda *refs: backward_kernel(dims, *refs), (places[chunk], mol_mode...]
    psum x2 -> x0, blocking collectives: 59.1 us -> none  [the longest x1 37.3 us: body(): lax.psum((grad_kw1, grad_cen, grad_wid, grad_g1, grad_b1, grad_g2, grad_b...]
    reduce_sum x18 -> x0, other arithmetic: 52.2 us -> none  [the longest x4 29.6 us: kernels(): offset = (place - centers) / widths]
    ppermute x0 -> x43, starting transfers between devices: none -> 47.7 us  [the longest x9 15.5 us: reduced(): got = lax.ppermute(sent, 'dp', flips(data, bit))]
    ppermute x0 -> x43, waiting for transfers between devices: none -> 47.2 us  [the longest x9 16 us: reduced(): got = lax.ppermute(sent, 'dp', flips(data, bit))]
    dynamic_update_slice x8 -> x2, local copies, waits for them, and re-layouts: 44.1 us -> 0.02 us  [the longest x1 0.01 us: body(): lax.dynamic_update_slice_in_dim(table, heads_of(tabs, 0, heads, pairs), t...]
  transfers between devices with their start and end apart: 5 -> 43, of which waited for: 3 -> 15; matrix products, arithmetic and copies ran while one was open for 32% -> 20% of each run, Pallas kernels for 0% -> 28%
where the time goes in v1:
time: 222 us; the launch traced here: 221 us
  Pallas kernels  71.9 us (32%)
  starting transfers between devices  47.7 us (21%)
  waiting for transfers between devices  47.2 us (21%)
  local copies, waits for them, and re-layouts  28.8 us (13%)
  other arithmetic  24.5 us (11%)
    pallas_call x2, Pallas kernels, body(): call(lambda *refs: backward_kernel(dims, *refs), (places[chunk], mol_mode...  24.2 us
    pallas_call x2, Pallas kernels, body(): call(lambda *refs: forward_kernel(dims, *refs), scalars, [row_block, vec,...  18.9 us
    ppermute x9, waiting for transfers between devices, reduced(): got = lax.ppermute(sent, 'dp', flips(data, bit))  16 us
    ppermute x9, starting transfers between devices, reduced(): got = lax.ppermute(sent, 'dp', flips(data, bit))  15.5 us
    ppermute x9, waiting for transfers between devices, reduced(): got = lax.ppermute(array, 'dp', flips(data, bit))  12.8 us
    ppermute x9, starting transfers between devices, reduced(): got = lax.ppermute(array, 'dp', flips(data, bit))  12.4 us
    ppermute x2, waiting for transfers between devices, body(): w2_full = w2_full + lax.ppermute(w2_full, 'tensor', flips(tensor, bit))  10.3 us
    pallas_call x2, Pallas kernels, body(): call(ffn_kernel, (places[chunk],), [row_block, act_block, act_block, row_...  9.27 us
  transfers between devices with their start and end apart: 43, of which 15 were waited for; matrix products, arithmetic and copies ran while one was open for 20% of the time, Pallas kernels for 28%

profile of v1, /device:TPU:0, one launch (start us, length us, event | category | flops | bytes accessed | tf_op | source)
XLA Modules:
  0.0 221.3 jit_solution(11482848264308498609)
XLA Ops:
  11.9 2.3 %copy.54.refs_7_.refs_10_ = bf16[3,768,192]{2,1,0:T(8,128)(2,1)} copy(bf16[3,768,192]{1,2,0:T(8,128)(2,1)} %collective-permute-done) | data formatting | bytes 1769472 | tf_op jit(solution)/shard_map/ppermute | solution.py:390
  14.9 9.4 %attend.3 = (bf16[256,768]{1,0:T(8,128)(2,1)}, bf16[256,768]{1,0:T(8,128)(2,1)}, bf16[6,256,192]{2,1,0:T(8,128)(2,1)}, bf16[2,256,192]{2,1,0:T(8,128)(2,1)}, bf16[4,2,256,128]{3,2,1,0:T(8,128)(2,1)}) custom-call(s32[2]{0:T(128)} %pad_add_fusion.2.refs_0_.where_ref, s32[16]{0:T(128)} %refs_1_.6, s32[16]{0:T(128)} %refs_1_.8, bf16[1024,768]{1,0:T(8,128)(2,1)} %refs_0_.8, ...), custom_call_target="tpu_custom_call" | custom-call | tf_op jit(solution)/shard_map/attend/pallas_call | solution.py:450
  24.3 2.6 %collective-permute-start.7 = (bf16[256,768]{1,0:T(8,128)(2,1)}, bf16[256,768]{1,0:T(8,128)(2,1)S(1)}, u32[]{:S(2)}, u32[]{:S(2)}) collective-permute-start(bf16[256,768]{1,0:T(8,128)(2,1)} %get-tuple-element.56.refs_1_), channel_id=1, source_target_pairs={{0,2},{1,3},{2,0},{3,1},{4,6},{5,7},{6,4},{7,5},{8,10},{9,11},{10,... | collective-permute-start | bytes 1179656 | tf_op jit(solution)/shard_map/ppermute | solution.py:394
  27.5 9.5 %attend.2 = (bf16[256,768]{1,0:T(8,128)(2,1)}, bf16[256,768]{1,0:T(8,128)(2,1)}, bf16[6,256,192]{2,1,0:T(8,128)(2,1)}, bf16[2,256,192]{2,1,0:T(8,128)(2,1)}, bf16[4,2,256,128]{3,2,1,0:T(8,128)(2,1)}) custom-call(s32[2]{0:T(128)} %pad_add_fusion.1.refs_0_.where_ref, s32[16]{0:T(128)} %refs_1_.6, s32[16]{0:T(128)} %refs_1_.8, bf16[1024,768]{1,0:T(8,128)(2,1)} %refs_0_.8, ...), custom_call_target="tpu_custom_call" | custom-call | tf_op jit(solution)/shard_map/attend/pallas_call | solution.py:450
  40.9 4.6 %ffn.3 = (f32[256,768]{1,0:T(8,128)}, bf16[256,768]{1,0:T(8,128)(2,1)}, bf16[4,256,192]{2,1,0:T(8,128)(2,1)}, bf16[256,768]{1,0:T(8,128)(2,1)}, bf16[256,768]{1,0:T(8,128)(2,1)}) custom-call(s32[2]{0:T(128)} %pad_add_fusion.2.refs_0_.where_ref, bf16[1024,768]{1,0:T(8,128)(2,1)} %refs_0_.8, bf16[256,768]{1,0:T(8,128)(2,1)} %get-tuple-element.56.refs_1_, ...), custom_call_target="tpu_custom_call" | custom-call | tf_op jit(solution)/shard_map/ffn/pallas_call | solution.py:470
  49.1 4.6 %ffn.2 = (f32[256,768]{1,0:T(8,128)}, bf16[256,768]{1,0:T(8,128)(2,1)}, bf16[4,256,192]{2,1,0:T(8,128)(2,1)}, bf16[256,768]{1,0:T(8,128)(2,1)}, bf16[256,768]{1,0:T(8,128)(2,1)}) custom-call(s32[2]{0:T(128)} %pad_add_fusion.1.refs_0_.where_ref, bf16[1024,768]{1,0:T(8,128)(2,1)} %refs_0_.8, bf16[256,768]{1,0:T(8,128)(2,1)} %get-tuple-element.53.refs_1_, ...), custom_call_target="tpu_custom_call" | custom-call | tf_op jit(solution)/shard_map/ffn/pallas_call | solution.py:470
  55.8 10.3 %collective-permute-done.42 = f32[32,128]{1,0:T(8,128)S(1)} collective-permute-done((f32[32,128]{1,0:T(8,128)S(1)}, f32[32,128]{1,0:T(8,128)S(1)}, u32[]{:S(2)}, u32[]{:S(2)}) %collective-permute-start.42) | collective-permute-done | bytes 16416 | tf_op jit(solution)/shard_map/ppermute | solution.py:567
  68.7 4.2 %ffn_grad.1 = bf16[2,2,192,768]{3,2,1,0:T(8,128)(2,1)} custom-call(s32[2]{0:T(128)} %pad_add_fusion.1.refs_0_.where_ref, bf16[1024,768]{1,0:T(8,128)(2,1)} %refs_1_.9, bf16[1024,768]{1,0:T(8,128)(2,1)} %refs_1_.9, bf16[256,768]{1,0:T(8,128)(2,1)} %get-tuple-element.79.refs_2_, bf16[256,768]{1,0:T(8,128)(2,1)} %get-tuple-element.80.refs_3_, ...), custom_call_target="tpu_custom_call" | custom-call | tf_op jit(solution)/shard_map/ffn_grad/pallas_call | solution.py:491
  72.9 2.3 %fusion.10 = (bf16[1,2,192,768]{3,2,1,0:T(8,128)(2,1)}, bf16[1,2,192,768]{3,2,1,0:T(8,128)(2,1)}) fusion(bf16[2,2,192,768]{3,2,1,0:T(8,128)(2,1)} %ffn_grad.1), kind=kLoop, calls=%fused_computation.72 | loop fusion | bytes 2359296 | tf_op jit(solution)/shard_map/slice | solution.py:541
  76.0 12.1 %attend_back.3 = (f32[256,768]{1,0:T(8,128)}, bf16[256,768]{1,0:T(8,128)(2,1)}, bf16[6,256,192]{2,1,0:T(8,128)(2,1)}, bf16[256,768]{1,0:T(8,128)(2,1)}, f32[4,768]{1,0:T(4,128)}, /*index=5*/f32[16,192]{1,0:T(8,128)}) custom-call(s32[2]{0:T(128)} %pad_add_fusion.2.refs_0_.where_ref, s32[16]{0:T(128)} %refs_1_.8, bf16[1024,768]{1,0:T(8,128)(2,1)} %refs_0_.8, ...), custom_call_target="tpu_custom_call" | custom-call | tf_op jit(solution)/shard_map/attend_back/pallas_call | solution.py:503
  90.6 12.1 %attend_back.2 = (f32[256,768]{1,0:T(8,128)}, bf16[256,768]{1,0:T(8,128)(2,1)}, bf16[6,256,192]{2,1,0:T(8,128)(2,1)}, bf16[256,768]{1,0:T(8,128)(2,1)}, f32[4,768]{1,0:T(4,128)}, /*index=5*/f32[16,192]{1,0:T(8,128)}) custom-call(s32[2]{0:T(128)} %pad_add_fusion.1.refs_0_.where_ref, s32[16]{0:T(128)} %refs_1_.8, bf16[1024,768]{1,0:T(8,128)(2,1)} %refs_0_.8, ...), custom_call_target="tpu_custom_call" | custom-call | tf_op jit(solution)/shard_map/attend_back/pallas_call | solution.py:503
  104.6 4.7 %proj_grad.1 = (bf16[2,3,192,768]{3,2,1,0:T(8,128)(2,1)}, bf16[2,192,768]{2,1,0:T(8,128)(2,1)}) custom-call(bf16[256,768]{1,0:T(8,128)(2,1)} %get-tuple-element.69.refs_0_, bf16[256,768]{1,0:T(8,128)(2,1)} %get-tuple-element.70.refs_1_, bf16[6,256,192]{2,1,0:T(8,128)(2,1)} %get-tuple-element.71.refs_2_, bf16[6,256,192]{2,1,0:T(8,128)(2,1)} %get-tuple-element.72.refs_3_, ...), custom_call_target="tpu_custom_call" | custom-call | tf_op jit(solution)/shard_map/proj_grad/pallas_call | solution.py:532
  109.3 2.6 %fusion.8 = (bf16[1,3,192,768]{3,2,1,0:T(8,128)(2,1)S(1)}, bf16[1,3,192,768]{3,2,1,0:T(8,128)(2,1)}) fusion(bf16[2,3,192,768]{3,2,1,0:T(8,128)(2,1)} %get-tuple-element.77), kind=kLoop, calls=%fused_computation.70 | loop fusion | bytes 3538944 | tf_op jit(solution)/shard_map/slice | solution.py:541
  113.0 3.1 %collective-permute-done.37 = f32[48,192]{1,0:T(8,128)S(1)} collective-permute-done((f32[48,192]{1,0:T(8,128)S(1)}, f32[48,192]{1,0:T(8,128)S(1)}, u32[]{:S(2)}, u32[]{:S(2)}) %collective-permute-start.37) | collective-permute-done | bytes 36896 | tf_op jit(solution)/shard_map/ppermute | solution.py:570
  120.6 1.9 collective-permute-start.39
  124.8 2.9 %collective-permute-start.40 = (f32[48,192]{1,0:T(8,128)S(1)}, f32[48,192]{1,0:T(8,128)S(1)}, u32[]{:S(2)}, u32[]{:S(2)}) collective-permute-start(f32[48,192]{1,0:T(8,128)S(1)} %add.199), channel_id=1, source_target_pairs={{0,16},{4,20},{8,24},{12,28},{16,0},{20,4},{24,8},{28,12},{1,17},{... | collective-permute-start | bytes 110600 | tf_op jit(solution)/shard_map/ppermute | solution.py:572
  130.5 2.0 kernel_net.1
  146.0 3.4 %finish.3 = bf16[256,768]{1,0:T(8,128)(2,1)} custom-call(s32[2]{0:T(128)} %pad_add_fusion.2.refs_0_.where_ref, bf16[1024,768]{1,0:T(8,128)(2,1)} %refs_0_.8, f32[256,768]{1,0:T(8,128)} %get-tuple-element.67.refs_1_, bf16[256,768]{1,0:T(8,128)(2,1)} %get-tuple-element.68.refs_2_, bf16[256,768]{1,0:T(8,128)(2,1)} %collective-permute-done.13.refs_3_, ...), custom_call_target="tpu_custom_call" | custom-call | tf_op jit(solution)/shard_map/finish/pallas_call | solution.py:585
  149.5 3.6 %finish.2 = bf16[256,768]{1,0:T(8,128)(2,1)} custom-call(s32[2]{0:T(128)} %pad_add_fusion.1.refs_0_.where_ref, bf16[1024,768]{1,0:T(8,128)(2,1)} %refs_0_.8, f32[256,768]{1,0:T(8,128)} %get-tuple-element.62.refs_1_, bf16[256,768]{1,0:T(8,128)(2,1)} %get-tuple-element.63.refs_2_, bf16[256,768]{1,0:T(8,128)(2,1)} %collective-permute-done.11.refs_3_, ...), custom_call_target="tpu_custom_call" | custom-call | tf_op jit(solution)/shard_map/finish/pallas_call | solution.py:585
  158.5 2.7 %collective-permute-start.25 = (bf16[24,768]{1,0:T(8,128)(2,1)S(1)}, bf16[24,768]{1,0:T(8,128)(2,1)S(1)}, u32[]{:S(2)}, u32[]{:S(2)}) collective-permute-start(bf16[24,768]{1,0:T(8,128)(2,1)S(1)} %constant_dynamic-slice_fusion.5), channel_id=1, source_target_pairs={{0,16},{4,20},{8,24},{12,28},{16,0},{20,4},{24,8},{28,12},{1,17},{... | collective-permute-start | bytes 110600 | tf_op jit(solution)/shard_map/ppermute | solution.py:547
  163.4 2.7 %collective-permute-start.26 = (bf16[24,768]{1,0:T(8,128)(2,1)S(1)}, bf16[24,768]{1,0:T(8,128)(2,1)S(1)}, u32[]{:S(2)}, u32[]{:S(2)}) collective-permute-start(bf16[24,768]{1,0:T(8,128)(2,1)S(1)} %add_convert_fusion.10), channel_id=1, source_target_pairs={{0,16},{4,20},{8,24},{12,28},{16,0},{20,4},{24,8},{28,12},{1,17},{... | collective-permute-start | bytes 110600 | tf_op jit(solution)/shard_map/ppermute | solution.py:550
  166.1 2.0 collective-permute-start.31
  172.9 3.2 %collective-permute-start.32 = (bf16[48,768]{1,0:T(8,128)(2,1)S(1)}, bf16[48,768]{1,0:T(8,128)(2,1)S(1)}, u32[]{:S(2)}, u32[]{:S(2)}) collective-permute-start(bf16[48,768]{1,0:T(8,128)(2,1)S(1)} %constant_dynamic-slice_fusion.2), channel_id=1, source_target_pairs={{0,16},{4,20},{8,24},{12,28},{16,0},{20,4},{24,8},{28,12},{1,17},{... | collective-permute-start | bytes 221192 | tf_op jit(solution)/shard_map/ppermute | solution.py:547
  177.0 4.9 %collective-permute-done.16 = bf16[288,768]{1,0:T(8,128)(2,1)S(1)} collective-permute-done((bf16[288,768]{1,0:T(8,128)(2,1)S(1)}, bf16[288,768]{1,0:T(8,128)(2,1)S(1)}, u32[]{:S(2)}, u32[]{:S(2)}) %collective-permute-start.16) | collective-permute-done | bytes 442400 | tf_op jit(solution)/shard_map/ppermute | solution.py:547
  182.7 2.9 %collective-permute-start.33 = (bf16[48,768]{1,0:T(8,128)(2,1)S(1)}, bf16[48,768]{1,0:T(8,128)(2,1)S(1)}, u32[]{:S(2)}, u32[]{:S(2)}) collective-permute-start(bf16[48,768]{1,0:T(8,128)(2,1)S(1)} %add_convert_fusion.8), channel_id=1, source_target_pairs={{0,16},{4,20},{8,24},{12,28},{16,0},{20,4},{24,8},{28,12},{1,17},{... | collective-permute-start | bytes 221192 | tf_op jit(solution)/shard_map/ppermute | solution.py:550
  185.5 5.8 %collective-permute-done.17 = bf16[144,768]{1,0:T(8,128)(2,1)S(1)} collective-permute-done((bf16[144,768]{1,0:T(8,128)(2,1)S(1)}, bf16[144,768]{1,0:T(8,128)(2,1)S(1)}, u32[]{:S(2)}, u32[]{:S(2)}) %collective-permute-start.17) | collective-permute-done | bytes 221216 | tf_op jit(solution)/shard_map/ppermute | solution.py:547
  193.1 2.5 %collective-permute-start.34 = (bf16[96,768]{1,0:T(8,128)(2,1)S(1)}, bf16[96,768]{1,0:T(8,128)(2,1)S(1)}, u32[]{:S(2)}, u32[]{:S(2)}) collective-permute-start(bf16[96,768]{1,0:T(8,128)(2,1)S(1)} %maximum_select_fusion.9), channel_id=1, source_target_pairs={{0,8},{4,12},{8,0},{12,4},{16,24},{20,28},{24,16},{28,20},{1,9},{5... | collective-permute-start | bytes 442376 | tf_op jit(solution)/shard_map/ppermute | solution.py:550
  195.7 2.4 %collective-permute-done.18 = bf16[72,768]{1,0:T(8,128)(2,1)S(1)} collective-permute-done((bf16[72,768]{1,0:T(8,128)(2,1)S(1)}, bf16[72,768]{1,0:T(8,128)(2,1)S(1)}, u32[]{:S(2)}, u32[]{:S(2)}) %collective-permute-start.18) | collective-permute-done | bytes 110624 | tf_op jit(solution)/shard_map/ppermute | solution.py:547
  199.6 3.1 %maximum_select_fusion = bf16[1024,768]{1,0:T(8,128)(2,1)} fusion(bf16[512,768]{1,0:T(8,128)(2,1)} %collective-permute-done.9, bf16[256,768]{1,0:T(8,128)(2,1)S(1)} %add_convert_fusion.1, bf16[256,768]{1,0:T(8,128)(2,1)S(1)} %add_convert_fusion.2, pred[]{:T(512)S(6)} %eq.10), kind=kLoop, calls=%fused_computation.3 | loop fusion | flops 10223616 | bytes 3145729 | tf_op jit(solution)/shard_map/jit(_where)/select_n | solution.py:600
  202.7 2.4 %collective-permute-done.19 = bf16[72,768]{1,0:T(8,128)(2,1)S(1)} collective-permute-done((bf16[72,768]{1,0:T(8,128)(2,1)S(1)}, bf16[72,768]{1,0:T(8,128)(2,1)S(1)}, u32[]{:S(2)}, u32[]{:S(2)}) %collective-permute-start.19) | collective-permute-done | bytes 110624 | tf_op jit(solution)/shard_map/ppermute | solution.py:550
  206.2 4.9 %collective-permute-done.20 = bf16[144,768]{1,0:T(8,128)(2,1)S(1)} collective-permute-done((bf16[144,768]{1,0:T(8,128)(2,1)S(1)}, bf16[144,768]{1,0:T(8,128)(2,1)S(1)}, u32[]{:S(2)}, u32[]{:S(2)}) %collective-permute-start.20) | collective-permute-done | bytes 221216 | tf_op jit(solution)/shard_map/ppermute | solution.py:550
  214.3 5.2 %collective-permute-done.21 = bf16[288,768]{1,0:T(8,128)(2,1)S(1)} collective-permute-done((bf16[288,768]{1,0:T(8,128)(2,1)S(1)}, bf16[288,768]{1,0:T(8,128)(2,1)S(1)}, u32[]{:S(2)}, u32[]{:S(2)}) %collective-permute-start.21) | collective-permute-done | bytes 442400 | tf_op jit(solution)/shard_map/ppermute | solution.py:550
  (217 shorter events, 77.2 us)
Async XLA Ops:
  2.8 11.4 %collective-permute-start.1 = (bf16[192,768]{1,0:T(8,128)(2,1)}, bf16[192,768]{1,0:T(8,128)(2,1)S(1)}, u32[]{:S(2)}, u32[]{:S(2)}) collective-permute-start(bf16[192,768]{1,0:T(8,128)(2,1)} %refs_11_.3), channel_id=1, source_target_pairs={{0,1},{1,0},{2,3},{3,2},{4,5},{5,4},{6,7},{7,6},{8,9},{9,8},{10,11... | collective-permute-start | bytes 884744 | tf_op jit(solution)/shard_map/ppermute | solution.py:390
  2.9 9.0 %collective-permute-start = (bf16[3,768,192]{1,2,0:T(8,128)(2,1)}, bf16[3,768,192]{1,2,0:T(8,128)(2,1)}, u32[]{:S(2)}, u32[]{:S(2)}) collective-permute-start(bf16[3,768,192]{1,2,0:T(8,128)(2,1)} %param.22), channel_id=1, source_target_pairs={{0,1},{1,0},{2,3},{3,2},{4,5},{5,4},{6,7},{7,6},{8,9},{9,8},{10,11... | collective-permute-start | bytes 2654216 | tf_op jit(solution)/shard_map/ppermute | solution.py:390
  24.3 15.0 %collective-permute-start.7 = (bf16[256,768]{1,0:T(8,128)(2,1)}, bf16[256,768]{1,0:T(8,128)(2,1)S(1)}, u32[]{:S(2)}, u32[]{:S(2)}) collective-permute-start(bf16[256,768]{1,0:T(8,128)(2,1)} %get-tuple-element.56.refs_1_), channel_id=1, source_target_pairs={{0,2},{1,3},{2,0},{3,1},{4,6},{5,7},{6,4},{7,5},{8,10},{9,11},{10,... | collective-permute-start | bytes 1179656 | tf_op jit(solution)/shard_map/ppermute | solution.py:394
  37.0 11.4 %collective-permute-start.3 = (bf16[256,768]{1,0:T(8,128)(2,1)}, bf16[256,768]{1,0:T(8,128)(2,1)S(1)}, u32[]{:S(2)}, u32[]{:S(2)}) collective-permute-start(bf16[256,768]{1,0:T(8,128)(2,1)} %get-tuple-element.53.refs_1_), channel_id=1, source_target_pairs={{0,2},{1,3},{2,0},{3,1},{4,6},{5,7},{6,4},{7,5},{8,10},{9,11},{10,... | collective-permute-start | bytes 1179656 | tf_op jit(solution)/shard_map/ppermute | solution.py:394
  37.9 16.2 %collective-permute-start.41 = (f32[32,128]{1,0:T(8,128)S(1)}, f32[32,128]{1,0:T(8,128)S(1)}, u32[]{:S(2)}, u32[]{:S(2)}) collective-permute-start(f32[32,128]{1,0:T(8,128)S(1)} %constant_dynamic-update-slice_fusion.1), channel_id=1, source_target_pairs={{0,1},{1,0},{2,3},{3,2},{4,5},{5,4},{6,7},{7,6},{8,9},{9,8},{10,11... | collective-permute-start | bytes 49160 | tf_op jit(solution)/shard_map/ppermute | solution.py:567
  45.5 29.7 %collective-permute-start.12 = (bf16[256,768]{1,0:T(8,128)(2,1)}, bf16[256,768]{1,0:T(8,128)(2,1)S(1)}, u32[]{:S(2)}, u32[]{:S(2)}) collective-permute-start(bf16[256,768]{1,0:T(8,128)(2,1)} %get-tuple-element.64.refs_5_), channel_id=1, source_target_pairs={{0,2},{1,3},{2,0},{3,1},{4,6},{5,7},{6,4},{7,5},{8,10},{9,11},{10,... | collective-permute-start | bytes 1179656 | tf_op jit(solution)/shard_map/ppermute | solution.py:394
  53.8 36.0 %collective-permute-start.10 = (bf16[256,768]{1,0:T(8,128)(2,1)}, bf16[256,768]{1,0:T(8,128)(2,1)S(1)}, u32[]{:S(2)}, u32[]{:S(2)}) collective-permute-start(bf16[256,768]{1,0:T(8,128)(2,1)} %get-tuple-element.59.refs_5_), channel_id=1, source_target_pairs={{0,2},{1,3},{2,0},{3,1},{4,6},{5,7},{6,4},{7,5},{8,10},{9,11},{10,... | collective-permute-start | bytes 1179656 | tf_op jit(solution)/shard_map/ppermute | solution.py:394
  54.1 12.0 %collective-permute-start.42 = (f32[32,128]{1,0:T(8,128)S(1)}, f32[32,128]{1,0:T(8,128)S(1)}, u32[]{:S(2)}, u32[]{:S(2)}) collective-permute-start(f32[32,128]{1,0:T(8,128)S(1)} %constant_dynamic-update-slice_fusion), channel_id=1, source_target_pairs={{0,2},{1,3},{2,0},{3,1},{4,6},{5,7},{6,4},{7,5},{8,10},{9,11},{10,... | collective-permute-start | bytes 49160 | tf_op jit(solution)/shard_map/ppermute | solution.py:567
  66.7 49.4 %collective-permute-start.8 = (bf16[256,768]{1,0:T(8,128)(2,1)S(1)}, bf16[256,768]{1,0:T(8,128)(2,1)}, u32[]{:S(2)}, u32[]{:S(2)}) collective-permute-start(bf16[256,768]{1,0:T(8,128)(2,1)S(1)} %copy-done.18), channel_id=1, source_target_pairs={{0,2},{1,3},{2,0},{3,1},{4,6},{5,7},{6,4},{7,5},{8,10},{9,11},{10,... | collective-permute-start | bytes 1179656 | tf_op jit(solution)/shard_map/ppermute | solution.py:394
  68.4 52.2 %collective-permute-start.6 = (bf16[256,768]{1,0:T(8,128)(2,1)}, bf16[256,768]{1,0:T(8,128)(2,1)}, u32[]{:S(2)}, u32[]{:S(2)}) collective-permute-start(bf16[256,768]{1,0:T(8,128)(2,1)} %get-tuple-element.55), channel_id=1, source_target_pairs={{0,2},{1,3},{2,0},{3,1},{4,6},{5,7},{6,4},{7,5},{8,10},{9,11},{10,... | collective-permute-start | bytes 1179656 | tf_op jit(solution)/shard_map/ppermute | solution.py:394
  75.2 66.2 %collective-permute-start.29 = (bf16[384,768]{1,0:T(8,128)(2,1)}, bf16[384,768]{1,0:T(8,128)(2,1)S(1)}, u32[]{:S(2)}, u32[]{:S(2)}) collective-permute-start(bf16[384,768]{1,0:T(8,128)(2,1)} %bitcast.17), channel_id=1, source_target_pairs={{0,1},{1,0},{2,3},{3,2},{4,5},{5,4},{6,7},{7,6},{8,9},{9,8},{10,11... | collective-permute-start | bytes 1769480 | tf_op jit(solution)/shard_map/ppermute | solution.py:390
  88.1 57.1 %collective-permute-start.13 = (bf16[256,768]{1,0:T(8,128)(2,1)}, bf16[256,768]{1,0:T(8,128)(2,1)}, u32[]{:S(2)}, u32[]{:S(2)}) collective-permute-start(bf16[256,768]{1,0:T(8,128)(2,1)} %get-tuple-element.68.refs_2_), channel_id=1, source_target_pairs={{0,2},{1,3},{2,0},{3,1},{4,6},{5,7},{6,4},{7,5},{8,10},{9,11},{10,... | collective-permute-start | bytes 1179656 | tf_op jit(solution)/shard_map/ppermute | solution.py:394
  104.3 7.6 %collective-permute-start.36 = (f32[48,192]{1,0:T(8,128)S(1)}, f32[48,192]{1,0:T(8,128)S(1)}, u32[]{:S(2)}, u32[]{:S(2)}) collective-permute-start(f32[48,192]{1,0:T(8,128)S(1)} %pad_maximum_fusion.2), channel_id=1, source_target_pairs={{0,1},{1,0},{2,3},{3,2},{4,5},{5,4},{6,7},{7,6},{8,9},{9,8},{10,11... | collective-permute-start | bytes 110600 | tf_op jit(solution)/shard_map/ppermute | solution.py:570
  116.1 22.3 %collective-permute-start.22 = (bf16[192,768]{1,0:T(8,128)(2,1)}, bf16[192,768]{1,0:T(8,128)(2,1)S(1)}, u32[]{:S(2)}, u32[]{:S(2)}) collective-permute-start(bf16[192,768]{1,0:T(8,128)(2,1)} %slice_bitcast_fusion.1), channel_id=1, source_target_pairs={{0,1},{1,0},{2,3},{3,2},{4,5},{5,4},{6,7},{7,6},{8,9},{9,8},{10,11... | collective-permute-start | bytes 884744 | tf_op jit(solution)/shard_map/ppermute | solution.py:390
  120.3 29.1 %collective-permute-start.11 = (bf16[256,768]{1,0:T(8,128)(2,1)}, bf16[256,768]{1,0:T(8,128)(2,1)}, u32[]{:S(2)}, u32[]{:S(2)}) collective-permute-start(bf16[256,768]{1,0:T(8,128)(2,1)} %get-tuple-element.63.refs_2_), channel_id=1, source_target_pairs={{0,2},{1,3},{2,0},{3,1},{4,6},{5,7},{6,4},{7,5},{8,10},{9,11},{10,... | collective-permute-start | bytes 1179656 | tf_op jit(solution)/shard_map/ppermute | solution.py:394
  129.8 69.7 %collective-permute-start.9 = (bf16[512,768]{1,0:T(8,128)(2,1)}, bf16[512,768]{1,0:T(8,128)(2,1)}, u32[]{:S(2)}, u32[]{:S(2)}) collective-permute-start(bf16[512,768]{1,0:T(8,128)(2,1)} %pad_maximum_fusion), channel_id=1, source_target_pairs={{0,1},{1,0},{2,3},{3,2},{4,5},{5,4},{6,7},{7,6},{8,9},{9,8},{10,11... | collective-permute-start | bytes 2359304 | tf_op jit(solution)/shard_map/ppermute | solution.py:390
  139.1 31.0 %collective-permute-start.15 = (bf16[576,768]{1,0:T(8,128)(2,1)}, bf16[576,768]{1,0:T(8,128)(2,1)}, u32[]{:S(2)}, u32[]{:S(2)}) collective-permute-start(bf16[576,768]{1,0:T(8,128)(2,1)} %bitcast.11), channel_id=1, source_target_pairs={{0,1},{1,0},{2,3},{3,2},{4,5},{5,4},{6,7},{7,6},{8,9},{9,8},{10,11... | collective-permute-start | bytes 2654216 | tf_op jit(solution)/shard_map/ppermute | solution.py:390
  141.4 11.7 %collective-permute-start.23 = (bf16[96,768]{1,0:T(8,128)(2,1)}, bf16[96,768]{1,0:T(8,128)(2,1)}, u32[]{:S(2)}, u32[]{:S(2)}) collective-permute-start(bf16[96,768]{1,0:T(8,128)(2,1)} %constant_dynamic-slice_fusion.7), channel_id=1, source_target_pairs={{0,4},{4,0},{8,12},{12,8},{16,20},{20,16},{24,28},{28,24},{1,5},{5... | collective-permute-start | bytes 442376 | tf_op jit(solution)/shard_map/ppermute | solution.py:547
  145.2 16.0 %collective-permute-start.30 = (bf16[192,768]{1,0:T(8,128)(2,1)}, bf16[192,768]{1,0:T(8,128)(2,1)}, u32[]{:S(2)}, u32[]{:S(2)}) collective-permute-start(bf16[192,768]{1,0:T(8,128)(2,1)} %constant_dynamic-slice_fusion.4), channel_id=1, source_target_pairs={{0,4},{4,0},{8,12},{12,8},{16,20},{20,16},{24,28},{28,24},{1,5},{5... | collective-permute-start | bytes 884744 | tf_op jit(solution)/shard_map/ppermute | solution.py:547
  156.7 54.6 %collective-permute-start.14 = (bf16[512,768]{1,0:T(8,128)(2,1)S(1)}, bf16[512,768]{1,0:T(8,128)(2,1)S(1)}, u32[]{:S(2)}, u32[]{:S(2)}) collective-permute-start(bf16[512,768]{1,0:T(8,128)(2,1)S(1)} %pad_maximum_fusion.1), channel_id=1, source_target_pairs={{0,1},{1,0},{2,3},{3,2},{4,5},{5,4},{6,7},{7,6},{8,9},{9,8},{10,11... | collective-permute-start | bytes 2359304 | tf_op jit(solution)/shard_map/ppermute | solution.py:390
  166.1 6.7 %collective-permute-start.31 = (bf16[96,768]{1,0:T(8,128)(2,1)S(1)}, bf16[96,768]{1,0:T(8,128)(2,1)S(1)}, u32[]{:S(2)}, u32[]{:S(2)}) collective-permute-start(bf16[96,768]{1,0:T(8,128)(2,1)S(1)} %constant_dynamic-slice_fusion.3), channel_id=1, source_target_pairs={{0,8},{4,12},{8,0},{12,4},{16,24},{20,28},{24,16},{28,20},{1,9},{5... | collective-permute-start | bytes 442376 | tf_op jit(solution)/shard_map/ppermute | solution.py:547
  168.5 7.6 %collective-permute-start.27 = (bf16[48,768]{1,0:T(8,128)(2,1)S(1)}, bf16[48,768]{1,0:T(8,128)(2,1)S(1)}, u32[]{:S(2)}, u32[]{:S(2)}) collective-permute-start(bf16[48,768]{1,0:T(8,128)(2,1)S(1)} %maximum_select_fusion.10), channel_id=1, source_target_pairs={{0,8},{4,12},{8,0},{12,4},{16,24},{20,28},{24,16},{28,20},{1,9},{5... | collective-permute-start | bytes 221192 | tf_op jit(solution)/shard_map/ppermute | solution.py:550
  171.5 10.4 %collective-permute-start.16 = (bf16[288,768]{1,0:T(8,128)(2,1)S(1)}, bf16[288,768]{1,0:T(8,128)(2,1)S(1)}, u32[]{:S(2)}, u32[]{:S(2)}) collective-permute-start(bf16[288,768]{1,0:T(8,128)(2,1)S(1)} %constant_dynamic-slice_fusion.10), channel_id=1, source_target_pairs={{0,4},{4,0},{8,12},{12,8},{16,20},{20,16},{24,28},{28,24},{1,5},{5... | collective-permute-start | bytes 1327112 | tf_op jit(solution)/shard_map/ppermute | solution.py:547
  172.9 9.8 %collective-permute-start.32 = (bf16[48,768]{1,0:T(8,128)(2,1)S(1)}, bf16[48,768]{1,0:T(8,128)(2,1)S(1)}, u32[]{:S(2)}, u32[]{:S(2)}) collective-permute-start(bf16[48,768]{1,0:T(8,128)(2,1)S(1)} %constant_dynamic-slice_fusion.2), channel_id=1, source_target_pairs={{0,16},{4,20},{8,24},{12,28},{16,0},{20,4},{24,8},{28,12},{1,17},{... | collective-permute-start | bytes 221192 | tf_op jit(solution)/shard_map/ppermute | solution.py:547
  176.1 29.1 %collective-permute-start.28 = (bf16[96,768]{1,0:T(8,128)(2,1)S(1)}, bf16[96,768]{1,0:T(8,128)(2,1)S(1)}, u32[]{:S(2)}, u32[]{:S(2)}) collective-permute-start(bf16[96,768]{1,0:T(8,128)(2,1)S(1)} %maximum_select_fusion.8), channel_id=1, source_target_pairs={{0,4},{4,0},{8,12},{12,8},{16,20},{20,16},{24,28},{28,24},{1,5},{5... | collective-permute-start | bytes 442376 | tf_op jit(solution)/shard_map/ppermute | solution.py:550
  182.1 9.3 %collective-permute-start.17 = (bf16[144,768]{1,0:T(8,128)(2,1)S(1)}, bf16[144,768]{1,0:T(8,128)(2,1)S(1)}, u32[]{:S(2)}, u32[]{:S(2)}) collective-permute-start(bf16[144,768]{1,0:T(8,128)(2,1)S(1)} %constant_dynamic-slice_fusion.9), channel_id=1, source_target_pairs={{0,8},{4,12},{8,0},{12,4},{16,24},{20,28},{24,16},{28,20},{1,9},{5... | collective-permute-start | bytes 663560 | tf_op jit(solution)/shard_map/ppermute | solution.py:547
  182.7 10.5 %collective-permute-start.33 = (bf16[48,768]{1,0:T(8,128)(2,1)S(1)}, bf16[48,768]{1,0:T(8,128)(2,1)S(1)}, u32[]{:S(2)}, u32[]{:S(2)}) collective-permute-start(bf16[48,768]{1,0:T(8,128)(2,1)S(1)} %add_convert_fusion.8), channel_id=1, source_target_pairs={{0,16},{4,20},{8,24},{12,28},{16,0},{20,4},{24,8},{28,12},{1,17},{... | collective-permute-start | bytes 221192 | tf_op jit(solution)/shard_map/ppermute | solution.py:550
  191.5 6.7 %collective-permute-start.18 = (bf16[72,768]{1,0:T(8,128)(2,1)S(1)}, bf16[72,768]{1,0:T(8,128)(2,1)S(1)}, u32[]{:S(2)}, u32[]{:S(2)}) collective-permute-start(bf16[72,768]{1,0:T(8,128)(2,1)S(1)} %constant_dynamic-slice_fusion.8), channel_id=1, source_target_pairs={{0,16},{4,20},{8,24},{12,28},{16,0},{20,4},{24,8},{28,12},{1,17},{... | collective-permute-start | bytes 331784 | tf_op jit(solution)/shard_map/ppermute | solution.py:547
  193.1 12.9 %collective-permute-start.34 = (bf16[96,768]{1,0:T(8,128)(2,1)S(1)}, bf16[96,768]{1,0:T(8,128)(2,1)S(1)}, u32[]{:S(2)}, u32[]{:S(2)}) collective-permute-start(bf16[96,768]{1,0:T(8,128)(2,1)S(1)} %maximum_select_fusion.9), channel_id=1, source_target_pairs={{0,8},{4,12},{8,0},{12,4},{16,24},{20,28},{24,16},{28,20},{1,9},{5... | collective-permute-start | bytes 442376 | tf_op jit(solution)/shard_map/ppermute | solution.py:550
  198.1 6.9 %collective-permute-start.19 = (bf16[72,768]{1,0:T(8,128)(2,1)S(1)}, bf16[72,768]{1,0:T(8,128)(2,1)S(1)}, u32[]{:S(2)}, u32[]{:S(2)}) collective-permute-start(bf16[72,768]{1,0:T(8,128)(2,1)S(1)} %add_convert_fusion.7), channel_id=1, source_target_pairs={{0,16},{4,20},{8,24},{12,28},{16,0},{20,4},{24,8},{28,12},{1,17},{... | collective-permute-start | bytes 331784 | tf_op jit(solution)/shard_map/ppermute | solution.py:550
  206.1 7.0 %collective-permute-start.35 = (bf16[192,768]{1,0:T(8,128)(2,1)S(1)}, bf16[192,768]{1,0:T(8,128)(2,1)S(1)}, u32[]{:S(2)}, u32[]{:S(2)}) collective-permute-start(bf16[192,768]{1,0:T(8,128)(2,1)S(1)} %maximum_select_fusion.6), channel_id=1, source_target_pairs={{0,4},{4,0},{8,12},{12,8},{16,20},{20,16},{24,28},{28,24},{1,5},{5... | collective-permute-start | bytes 884744 | tf_op jit(solution)/shard_map/ppermute | solution.py:550
  211.2 8.4 %collective-permute-start.21 = (bf16[288,768]{1,0:T(8,128)(2,1)S(1)}, bf16[288,768]{1,0:T(8,128)(2,1)S(1)}, u32[]{:S(2)}, u32[]{:S(2)}) collective-permute-start(bf16[288,768]{1,0:T(8,128)(2,1)S(1)} %maximum_select_fusion.4), channel_id=1, source_target_pairs={{0,4},{4,0},{8,12},{12,8},{16,20},{20,16},{24,28},{28,24},{1,5},{5... | collective-permute-start | bytes 1327112 | tf_op jit(solution)/shard_map/ppermute | solution.py:550
  (39 other events, 214.2 us)
